TPU v7x, 32 devices: a whole 2x2x4 slice. The times are simulated.
32 devices in a mesh: members: 2 (over y), lat: 4 (over z), lon: 2 (over x), chan: 2 (over core).
Axes of the slice: x: 2, y: 2, z: 4, core: 2. Of those that a mesh axis runs over, the one named last changes fastest.
Arguments:
- atmos_state: float32 [768, 96, 384], P(('members', 'lon', 'chan'), 'lat'), parts along dimension 0, may hold values from -6 to 6
- ocean_state: float32 [400, 16, 512], P('members', 'lat', ('lon', 'chan')), parts along dimension 0, may hold values from -6 to 6
- land_mask: int32 [16, 512], P('lat', ('lon', 'chan')), may hold values from 0 to 1, as said below
- spectral_filter: float32 [2, 384, 384, 96], P(None, ('lon', 'chan'), 'lat'), may hold values from -6 to 6
- atmos_gain: float32 [384], P(('lon', 'chan')), may hold values from 0.1 to 1.9
- flux_readout: float32 [8, 384], P(None, ('lon', 'chan')), may hold values from -0.3125 to 0.3125
- surface_coupling: float32 [384, 4], P(('lon', 'chan')), may hold values from -3 to 3
- surface_readout: float32 [4, 200], replicated, may hold values from -0.4375 to 0.4375
- flux_coupling: float32 [200, 8], replicated, may hold values from -2 to 2
- atmos_row_source: int32 [96, 2], P('lat'), may hold values from 0 to 15, as said below
- atmos_row_weight: float32 [96, 2], P('lat'), may hold values from 0.2 to 1
- atmos_col_source: int32 [384, 2], P(('lon', 'chan')), may hold values from 0 to 511, as said below
- atmos_col_weight: float32 [384, 2], P(('lon', 'chan')), may hold values from 0.2 to 1
- ocean_row_source: int32 [16, 2], P('lat'), may hold values from 0 to 95, as said below
- ocean_row_weight: float32 [16, 2], P('lat'), may hold values from 0.2 to 1
- ocean_col_source: int32 [512, 2], P(('lon', 'chan')), may hold values from 0 to 383, as said below
- ocean_col_weight: float32 [512, 2], P(('lon', 'chan')), may hold values from 0.2 to 1
- depth_taps: float32 [2, 200, 9], replicated, may hold values from -2 to 2
- block_gain: float32 [2, 200], replicated, may hold values from 0.1 to 1.9
- expand_weight: float32 [2, 200, 800], replicated, may hold values from -0.4375 to 0.4375
- reduce_weight: float32 [2, 800, 200], replicated, may hold values from -0.21875 to 0.21875
- layer_scale: float32 [2, 200], replicated, may hold values from 0.1 to 1.9
Outputs:
- atmos_next: float32 [768, 96, 384], P(('members', 'lon', 'chan'), 'lat'), parts along dimension 0
- ocean_next: float32 [400, 16, 512], P('members', 'lat', ('lon', 'chan')), parts along dimension 0
There are 2 independent parts, one for each index of `members`. A program takes and returns all parts, laid end to end along the dimension named above; an argument that names none is the same for every part. Nothing has to cross between parts.
Inputs may be any that keep to these rules, and one draw needn't show every extreme that they name: `atmos_row_source`: row t holds b and b + 1, where b - (16 * t) // 96 is -1, 0 or 1 before b is clipped to 0 .. 14; the offsets -1 and 1 both occur. `atmos_col_source`: row t holds b mod 512 and (b + 1) mod 512, where b - (512 * t) // 384 is -1, 0 or 1; the offsets -1 and 1 both occur. `ocean_row_source`: row t holds b and b + 1, where b - (96 * t) // 16 is -1, 0 or 1 before b is clipped to 0 .. 94; the offsets -1 and 1 both occur. `ocean_col_source`: row t holds b mod 384 and (b + 1) mod 384, where b - (384 * t) // 512 is -1, 0 or 1; the offsets -1 and 1 both occur. `land_mask`: the first and last latitude rows are land.
All inputs are finite; a program needn't handle non-finite values.
Results may differ from a plain program's by a relative error of at most 0.0001.
Values sent between devices are 32-bit elements; how exact they have to be, the bound alone decides.
A program may use at most 128 MiB of HBM per device.

v0:
```python
import functools
import math

import jax
import jax.numpy as jnp
from jax import lax
from jax.experimental import pallas as pl
from jax.experimental.pallas import tpu as pltpu
from jax.sharding import PartitionSpec as P

CA = 384


EPSILON = 1e-05
PRECISE = lax.Precision.HIGH
EXACT = lax.Precision.HIGHEST
LANES = 128
PACK = 4
TABLE_ROWS = 16


def padded(x, sides, width):
    for axis, dim in sides:
        count, length = (lax.axis_size(axis), x.shape[dim])
        up = [(i, (i + 1) % count) for i in range(count)]
        down = [(j, i) for i, j in up]
        last = lax.slice_in_dim(x, length - width, length, axis=dim)
        leading = lax.slice_in_dim(x, 0, width, axis=dim)
        before = lax.ppermute(last, axis, up)
        after = lax.ppermute(leading, axis, down)
        x = jnp.concatenate([before, x, after], axis=dim)
    return x


def fourier_tables(length):
    places = jnp.arange(length, dtype=jnp.int32)
    angles = (
        2.0
        * math.pi
        / length
        * jnp.mod(places[:, None] * places[None, :], length).astype(jnp.float32)
    )
    return (jnp.cos(angles), jnp.sin(angles))


def regrid_matrix(source, weight, offset, span, period):
    shares = weight / jnp.sum(weight, axis=1, keepdims=True)
    relative = source - offset
    if period > 0:
        relative = jnp.mod(relative, period)
    columns = jnp.arange(span, dtype=relative.dtype)[None, :]
    return shares[:, 0:1] * (relative[:, 0:1] == columns).astype(jnp.float32) + shares[:, 1:2] * (
        relative[:, 1:2] == columns
    ).astype(jnp.float32)


def apply_maps(field, row_map, col_map):
    by_rows = jnp.einsum("jh,shw->sjw", row_map, field, precision=PRECISE)
    return jnp.einsum("sjw,kw->sjk", by_rows, col_map, precision=PRECISE)


def grid_rims(field):
    return padded(field, (("lat", 1), (("lon", "chan"), 2)), 2)


def along_last(field, table):
    return jnp.einsum("ckh,hm->ckm", field, table, precision=PRECISE)


def global_filter(normed, spectral_filter):
    width_len = normed.shape[2]
    height_len = spectral_filter.shape[3]
    cos_w, sin_w = fourier_tables(width_len)
    cos_h, sin_h = fourier_tables(height_len)
    real_w = jnp.einsum("chn,nk->ckh", normed, cos_w, precision=PRECISE)
    imag_w = -jnp.einsum("chn,nk->ckh", normed, sin_w, precision=PRECISE)
    real_w, imag_w = (
        lax.all_to_all(real_w, "lat", split_axis=1, concat_axis=2, tiled=True),
        lax.all_to_all(imag_w, "lat", split_axis=1, concat_axis=2, tiled=True),
    )
    real_s = along_last(real_w, cos_h) + along_last(imag_w, sin_h)
    imag_s = along_last(imag_w, cos_h) - along_last(real_w, sin_h)
    kern_real = spectral_filter[0]
    kern_imag = spectral_filter[1]
    real_f = kern_real * real_s - kern_imag * imag_s
    imag_f = kern_real * imag_s + kern_imag * real_s
    real_b = (along_last(real_f, cos_h) - along_last(imag_f, sin_h)) / height_len
    imag_b = (along_last(imag_f, cos_h) + along_last(real_f, sin_h)) / height_len
    real_b, imag_b = (
        lax.all_to_all(real_b, "lat", split_axis=2, concat_axis=1, tiled=True),
        lax.all_to_all(imag_b, "lat", split_axis=2, concat_axis=1, tiled=True),
    )
    back = jnp.einsum("ckh,kn->chn", real_b, cos_w, precision=PRECISE) - jnp.einsum(
        "ckh,kn->chn", imag_b, sin_w, precision=PRECISE
    )
    return back / width_len


def split_value(x):
    high = x.astype(jnp.bfloat16)
    return high, (x - high.astype(jnp.float32)).astype(jnp.bfloat16)


def wave(rows, columns, length):
    steps = lax.rem(rows * columns, length)
    angles = (2.0 * math.pi / length) * steps.astype(jnp.float32)
    return jnp.cos(angles), jnp.sin(angles)


def fill_tables(w_hi, w_lo, f_hi, f_lo, b_hi, b_lo):
    width, height = w_hi.shape[0], f_hi.shape[0] // 2

    def places(block, columns):
        shape = (TABLE_ROWS, columns)
        rows = lax.broadcasted_iota(jnp.int32, shape, 0) + block * TABLE_ROWS
        return rows, lax.broadcasted_iota(jnp.int32, shape, 1)

    def span(block):
        return pl.ds(pl.multiple_of(block * TABLE_ROWS, TABLE_ROWS), TABLE_ROWS)

    def along_width(block, carry):
        cos_w, sin_w = wave(*places(block, width), width)
        w_hi[span(block), :width], w_lo[span(block), :width] = split_value(cos_w)
        w_hi[span(block), width:], w_lo[span(block), width:] = split_value(-sin_w)
        return carry

    def along_height(block, carry):
        rows, columns = places(block, 2 * height)
        lower, right = rows >= height, columns >= height
        cos_h, sin_h = wave(
            jnp.where(lower, rows - height, rows), jnp.where(right, columns - height, columns), height
        )
        level = lower == right
        forward = jnp.where(level, cos_h, jnp.where(right, sin_h, -sin_h))
        inverse = jnp.where(level, cos_h, jnp.where(right, -sin_h, sin_h)) / (height * width)
        f_hi[span(block), :], f_lo[span(block), :] = split_value(forward)
        b_hi[span(block), :], b_lo[span(block), :] = split_value(inverse)
        return carry

    lax.fori_loop(0, width // TABLE_ROWS, along_width, 0)
    lax.fori_loop(0, 2 * height // TABLE_ROWS, along_height, 0)


def product(left, right):
    dot = functools.partial(jnp.dot, preferred_element_type=jnp.float32)
    return dot(left[0], right[0]) + (dot(left[0], right[1]) + dot(left[1], right[0]))


def pack_kernel(member_ref, filter_ref, packed_ref):
    del member_ref
    piece = LANES // PACK
    for part in range(filter_ref.shape[0]):
        last = filter_ref[part, 0, 0, 0, PACK - 1]
        for j in range(PACK - 1):
            packed_ref[0, part, 0, j] = jnp.concatenate(
                [filter_ref[part, 0, 0, 0, j], last[:, piece * j : piece * (j + 1)]],
                axis=1,
            )


def pack_filter(spectral_filter, lat_count, members, first, count):
    parts, channels, freqs, height_len = spectral_filter.shape
    groups = channels // (lat_count * members * PACK)
    member = lax.axis_index("members").astype(jnp.int32).reshape(1)
    split = spectral_filter.reshape(parts, lat_count, members, groups, PACK, freqs, height_len)
    return pl.pallas_call(
        pack_kernel,
        out_shape=jax.ShapeDtypeStruct(
            (lat_count, parts, count, PACK - 1, freqs, LANES), jnp.float32
        ),
        grid_spec=pltpu.PrefetchScalarGridSpec(
            num_scalar_prefetch=1,
            grid=(lat_count, count),
            in_specs=[
                pl.BlockSpec(
                    (parts, 1, 1, 1, PACK, freqs, height_len),
                    lambda i, g, m: (0, i, m[0], g + first, 0, 0, 0),
                )
            ],
            out_specs=pl.BlockSpec(
                (1, parts, 1, PACK - 1, freqs, LANES), lambda i, g, m: (i, 0, g, 0, 0, 0)
            ),
        ),
        cost_estimate=pl.CostEstimate(
            flops=0,
            transcendentals=0,
            bytes_accessed=6 * spectral_filter.size * count // groups,
        ),
    )(member, split)


def filter_group(x_ref, filter_ref, tables, out_ref, wide_ref):
    blocks, _, block_rows, width = x_ref.shape
    height = blocks * block_rows
    w_hi, w_lo, f_hi, f_lo, b_hi, b_lo = tables
    table_w = (w_hi[...], w_lo[...])
    forward = (f_hi[...], f_lo[...])
    inverse = (b_hi[...], b_lo[...])
    rows = jnp.concatenate([x_ref[:, j].reshape(height, width) for j in range(PACK)], axis=0)
    spectra = product(split_value(rows), table_w)
    packed = [
        [filter_ref[:, part, j].reshape(width, LANES).T for j in range(PACK - 1)]
        for part in range(2)
    ]
    kernels = [
        [p[:height] for p in of_part] + [jnp.concatenate([p[height:] for p in of_part], axis=0)]
        for of_part in packed
    ]
    for j in range(PACK):
        own = spectra[height * j : height * (j + 1)]
        stacked = jnp.concatenate([own[:, :width], own[:, width:]], axis=0)
        full = product(forward, split_value(stacked))
        real_s, imag_s = full[:height], full[height:]
        real_k, imag_k = kernels[0][j], kernels[1][j]
        filtered = jnp.concatenate(
            [real_k * real_s - imag_k * imag_s, real_k * imag_s + imag_k * real_s], axis=0
        )
        back = product(inverse, split_value(filtered))
        wide_ref[height * j : height * (j + 1), :width] = back[:height]
        wide_ref[height * j : height * (j + 1), width:] = back[height:]
    wide = split_value(wide_ref[...])
    result = product(
        (wide[0][:, :width], wide[1][:, :width]), (table_w[0][:, :width], table_w[1][:, :width])
    ) + product(
        (wide[0][:, width:], wide[1][:, width:]), (table_w[0][:, width:], table_w[1][:, width:])
    )
    for j in range(PACK):
        own = result[height * j : height * (j + 1)]
        out_ref[:, j] = own.reshape(blocks, block_rows, width)


def spectral_kernel(
    normed_ref, first_ref, rest_ref, out_ref,
    kernels_ref, arrived_ref, back_ref, wide_ref, w_hi, w_lo, f_hi, f_lo, b_hi, b_lo,
    go_send, go_recv, go_local, come_send, come_recv, come_local, swap_send, swap_recv, own_sem,
):
    count = normed_ref.shape[0]
    steps = arrived_ref.shape[0]
    groups = steps // 2
    me = lax.axis_index("lat")
    member = lax.axis_index("members")
    peers = [(k, lax.rem(me + k, count)) for k in range(1, count)]
    barrier = pltpu.get_barrier_semaphore()
    for _, peer in peers:
        pl.semaphore_signal(
            barrier, inc=1, device_id={"lat": peer}, device_id_type=pl.DeviceIdType.MESH
        )
    pl.semaphore_signal(
        barrier, inc=1, device_id={"members": 1 - member}, device_id_type=pl.DeviceIdType.MESH
    )

    def place(step):
        second = step // groups
        return member + second - 2 * member * second, pl.ds(PACK * (step % groups), PACK)

    def going(step, k, peer):
        half, span = place(step)
        return pltpu.make_async_remote_copy(
            src_ref=normed_ref.at[peer, half, span],
            dst_ref=arrived_ref.at[step, me],
            send_sem=go_send.at[step, k - 1],
            recv_sem=go_recv.at[step, k - 1],
            device_id={"lat": peer},
            device_id_type=pl.DeviceIdType.MESH,
        )

    def staying(step):
        half, span = place(step)
        return pltpu.make_async_copy(
            normed_ref.at[me, half, span], arrived_ref.at[step, me], go_local.at[step]
        )

    def coming(step, k, peer):
        half, span = place(step)
        return pltpu.make_async_remote_copy(
            src_ref=back_ref.at[step, peer],
            dst_ref=out_ref.at[me, half, span],
            send_sem=come_send.at[step, k - 1],
            recv_sem=come_recv.at[step, k - 1],
            device_id={"lat": peer},
            device_id_type=pl.DeviceIdType.MESH,
        )

    def kept(step):
        half, span = place(step)
        return pltpu.make_async_copy(
            back_ref.at[step, me], out_ref.at[me, half, span], come_local.at[step]
        )

    def held(group):
        begun = first_ref.shape[2]
        return first_ref.at[:, :, group] if group < begun else rest_ref.at[:, :, group - begun]

    def own_filter(group):
        return pltpu.make_async_copy(held(group), kernels_ref.at[group], own_sem.at[group])

    def swapped(group):
        return pltpu.make_async_remote_copy(
            src_ref=held(group),
            dst_ref=kernels_ref.at[groups + group],
            send_sem=swap_send.at[group],
            recv_sem=swap_recv.at[group],
            device_id={"members": 1 - member},
            device_id_type=pl.DeviceIdType.MESH,
        )

    pl.semaphore_wait(barrier, count)
    for step in range(steps):
        for k, peer in peers:
            going(step, k, peer).start()
        staying(step).start()
        if step < groups:
            own_filter(step).start()
            swapped(step).start()

    fill_tables(w_hi, w_lo, f_hi, f_lo, b_hi, b_lo)

    def one_step(step, carry):
        staying(step).wait()
        for k, peer in peers:
            going(step, k, peer).wait_recv()

        for group in range(groups):

            @pl.when(step == group)
            def _():
                own_filter(group).wait()

            @pl.when(step == groups + group)
            def _():
                swapped(group).wait_recv()

        filter_group(
            arrived_ref.at[step],
            kernels_ref.at[step],
            (w_hi, w_lo, f_hi, f_lo, b_hi, b_lo),
            back_ref.at[step],
            wide_ref,
        )
        for k, peer in peers:
            coming(step, k, peer).start()
        kept(step).start()
        return carry

    lax.fori_loop(0, steps, one_step, 0)
    for group in range(groups):
        swapped(group).wait_send()
    for step in range(steps):
        kept(step).wait()
        for k, peer in peers:
            going(step, k, peer).wait_send()
            coming(step, k, peer).wait()


def spectral_step(normed, first, rest):
    lat_count, halves, _, rows, width = normed.shape
    parts, groups = first.shape[1], first.shape[2] + rest.shape[2]
    height = lat_count * rows
    steps = halves * groups
    anywhere = pl.BlockSpec(memory_space=pl.ANY)
    dma = pltpu.SemaphoreType.DMA
    tables = [(width, 2 * width)] * 2 + [(2 * height, 2 * height)] * 4
    return pl.pallas_call(
        spectral_kernel,
        out_shape=jax.ShapeDtypeStruct(normed.shape, jnp.float32),
        in_specs=[anywhere] * 3,
        out_specs=anywhere,
        scratch_shapes=[
            pltpu.VMEM((steps, lat_count, parts) + first.shape[3:], jnp.float32),
            pltpu.VMEM((steps, lat_count, PACK, rows, width), jnp.float32),
            pltpu.VMEM((steps, lat_count, PACK, rows, width), jnp.float32),
            pltpu.VMEM((PACK * height, 2 * width), jnp.float32),
            *(pltpu.VMEM(shape, jnp.bfloat16) for shape in tables),
            dma((steps, lat_count - 1)),
            dma((steps, lat_count - 1)),
            dma((steps,)),
            dma((steps, lat_count - 1)),
            dma((steps, lat_count - 1)),
            dma((steps,)),
            dma((groups,)),
            dma((groups,)),
            dma((groups,)),
        ],
        compiler_params=pltpu.CompilerParams(collective_id=1, has_side_effects=True),
        cost_estimate=pl.CostEstimate(
            flops=12 * steps * PACK * height * width * (2 * width + 2 * height),
            transcendentals=0,
            bytes_accessed=8 * normed.size + 4 * (first.size + rest.size),
        ),
    )(normed, first, rest)


def exchanged(x):
    return lax.all_to_all(x, "lat", split_axis=0, concat_axis=0, tiled=True)


def summed(x, axes):
    for axis in axes:
        if lax.axis_size(axis) == 2:
            x = x + lax.ppermute(x, axis, [(0, 1), (1, 0)])
        else:
            x = lax.psum(x, axis)
    return x


def channels_divide(atmos_state, spectral_filter, ocean_rows, ocean_cols):
    channels, rows, width = atmos_state.shape
    height = spectral_filter.shape[3]
    unit = lax.axis_size("lat") * lax.axis_size("members") * PACK
    return (
        channels % unit == 0
        and lax.axis_size("members") == 2
        and rows % 8 == 0
        and width % LANES == 0
        and PACK * height == (PACK - 1) * LANES
        and spectral_filter.shape[2] % 8 == 0
        and (lax.axis_size("lat") * rows) % TABLE_ROWS == 0
        and width % TABLE_ROWS == 0
        and channels > unit
        and width >= ocean_cols
        and rows % ocean_rows == 0
        and ocean_rows >= 4
        and rows // ocean_rows >= 3
    )


def depthwise(field, taps):
    height = field.shape[1] - 2
    width = field.shape[2] - 2
    result = jnp.zeros((field.shape[0], height, width), jnp.float32)
    for row_off in range(3):
        for col_off in range(3):
            result = (
                result
                + taps[:, 3 * row_off + col_off][:, None, None]
                * field[:, row_off : row_off + height, col_off : col_off + width]
            )
    return result


def ocean_mixer(values, gain, expand, reduce_w):
    channels, height, width = values.shape
    flat = values.reshape(channels, height * width)
    centre = jnp.mean(flat, axis=0)
    spread = jnp.mean(flat * flat, axis=0) - centre * centre
    normed = (flat - centre) * lax.rsqrt(spread + EPSILON) * gain[:, None]
    hidden = jax.nn.gelu(jnp.einsum("cd,cp->dp", expand, normed, precision=PRECISE))
    update = jnp.einsum("dc,dp->cp", reduce_w, hidden, precision=PRECISE)
    return update.reshape(channels, height, width)


def by_frequencies(
    atmos_state,
    ocean_state,
    land_mask,
    spectral_filter,
    atmos_gain,
    flux_readout,
    surface_coupling,
    surface_readout,
    flux_coupling,
    to_atmos,
    to_ocean,
    depth_taps,
    block_gain,
    expand_weight,
    reduce_weight,
    layer_scale,
):
    atmos_row_source, atmos_row_weight, atmos_col_source, atmos_col_weight = to_atmos
    ocean_row_source, ocean_row_weight, ocean_col_source, ocean_col_weight = to_ocean
    atm_rows = atmos_state.shape[1]
    width_atm = atmos_state.shape[2]
    ocean_rows = ocean_state.shape[1]
    ocean_cols = ocean_state.shape[2]
    col_groups = lax.axis_size(("lon", "chan"))
    atm_cols = width_atm // col_groups
    lat_place = lax.axis_index("lat")
    col_place = lax.axis_index(("lon", "chan"))
    partial_flux = jnp.einsum("fc,chw->fhw", flux_readout, atmos_state, precision=PRECISE)
    flux_full, column_sum, square_sum = lax.psum(
        (partial_flux, jnp.sum(atmos_state, axis=0), jnp.sum(atmos_state * atmos_state, axis=0)),
        ("lon", "chan"),
    )
    centre = column_sum / CA
    spread = square_sum / CA - centre * centre
    scale = lax.rsqrt(spread + EPSILON)
    normed = (atmos_state - centre) * scale * atmos_gain[:, None, None]
    filtered = global_filter(normed, spectral_filter)
    surface = jnp.einsum("sc,chw->shw", surface_readout, ocean_state, precision=PRECISE)
    surface_rim = grid_rims(surface)
    row_map = regrid_matrix(
        atmos_row_source, atmos_row_weight, lat_place * ocean_rows - 2, ocean_rows + 4, 0
    )
    col_map = regrid_matrix(
        atmos_col_source,
        atmos_col_weight,
        col_place * ocean_cols - 2,
        ocean_cols + 4,
        ocean_cols * col_groups,
    )
    atmos_piece = apply_maps(surface_rim, row_map, col_map)
    forcing = jnp.einsum(
        "cs,shw->chw",
        surface_coupling,
        lax.all_gather(atmos_piece, ("lon", "chan"), axis=2, tiled=True),
        precision=PRECISE,
    )
    atmos_next = atmos_state + filtered + forcing
    flux_cols = lax.dynamic_slice_in_dim(flux_full, col_place * atm_cols, atm_cols, 2)
    flux_rim = grid_rims(flux_cols)
    row_back = regrid_matrix(
        ocean_row_source, ocean_row_weight, lat_place * atm_rows - 2, atm_rows + 4, 0
    )
    col_back = regrid_matrix(
        ocean_col_source, ocean_col_weight, col_place * atm_cols - 2, atm_cols + 4, width_atm
    )
    flux_ocean = apply_maps(flux_rim, row_back, col_back)
    ocean_mask = land_mask.astype(jnp.float32)
    current = ocean_mask * (
        ocean_state + jnp.einsum("cf,fhw->chw", flux_coupling, flux_ocean, precision=PRECISE)
    )
    padded_field = grid_rims(current)
    mask_padded = grid_rims(ocean_mask[None])[0]
    update = ocean_mixer(
        depthwise(padded_field, depth_taps[0]), block_gain[0], expand_weight[0], reduce_weight[0]
    )
    widened = mask_padded[1:-1, 1:-1] * (
        padded_field[:, 1:-1, 1:-1] + layer_scale[0][:, None, None] * update
    )
    update = ocean_mixer(
        depthwise(widened, depth_taps[1]), block_gain[1], expand_weight[1], reduce_weight[1]
    )
    current = ocean_mask * (widened[:, 1:-1, 1:-1] + layer_scale[1][:, None, None] * update)
    return (atmos_next, current)


def by_channels(
    atmos_state,
    ocean_state,
    land_mask,
    spectral_filter,
    atmos_gain,
    flux_readout,
    surface_coupling,
    surface_readout,
    flux_coupling,
    to_atmos,
    to_ocean,
    depth_taps,
    block_gain,
    expand_weight,
    reduce_weight,
    layer_scale,
):
    channels, atm_rows, width_atm = atmos_state.shape
    ocean_channels, ocean_rows, ocean_cols = ocean_state.shape
    fields = surface_readout.shape[0]
    fluxes = flux_readout.shape[0]
    col_groups = lax.axis_size(("lon", "chan"))
    atm_cols = width_atm // col_groups
    lat_count = lax.axis_size("lat")
    lat_place = lax.axis_index("lat")
    col_place = lax.axis_index(("lon", "chan"))
    hold = lax.optimization_barrier

    mask = land_mask.astype(jnp.float32)
    groups = channels // (lat_count * 2 * PACK)
    packed_first = pack_filter(spectral_filter, lat_count, 2, 0, 1)
    packed_first, ocean_state, atmos_state = hold((packed_first, ocean_state, atmos_state))
    kernels_first = exchanged(packed_first)
    packed_rest = pack_filter(spectral_filter, lat_count, 2, 1, groups - 1)
    up = [(i, (i + 1) % lat_count) for i in range(lat_count)]
    down = [(j, i) for i, j in up]
    partial_flux = jnp.einsum("fc,chw->fhw", flux_readout, atmos_state, precision=EXACT)
    own_rows = regrid_matrix(to_ocean[0], to_ocean[1], lat_place * atm_rows - 1, atm_rows + 1, 0)
    by_rows = jnp.einsum("jh,fhw->fjw", own_rows[:, 1:], partial_flux, precision=PRECISE)
    weight_up = own_rows[0, 0]
    closing = partial_flux[:, -1:]

    def with_mask(rows, edge):
        edge = jnp.pad(edge, ((0, 1), (0, width_atm - ocean_cols)))
        return jnp.concatenate([rows, edge[None]], axis=0)

    to_below = with_mask(jnp.concatenate([by_rows[:, -2:], closing], axis=1), mask[-2:])
    to_above = with_mask(
        jnp.concatenate([by_rows[:, :2], jnp.broadcast_to(weight_up, closing.shape)], axis=1),
        mask[:2],
    )
    rows_before = lax.ppermute(ocean_state[:, -2:], "lat", up)
    rows_after = lax.ppermute(ocean_state[:, :2], "lat", down)
    from_above = lax.ppermute(to_below, "lat", up)
    from_below = lax.ppermute(to_above, "lat", down)
    kernels_rest = exchanged(packed_rest)
    mask_above, mask_below = from_above[fluxes, :2, :ocean_cols], from_below[fluxes, :2, :ocean_cols]
    from_above, from_below = from_above[:fluxes], from_below[:fluxes]

    flux_rows = jnp.concatenate(
        [
            from_above[:, :2],
            by_rows[:, :1] + weight_up * from_above[:, 2:],
            by_rows[:, 1:],
            from_below[:, :1] + from_below[:, 2:] * closing,
            from_below[:, 1:2],
        ],
        axis=1,
    )
    sums = jnp.stack([jnp.sum(atmos_state, axis=0), jnp.sum(atmos_state * atmos_state, axis=0)])
    ext_rows = flux_rows.shape[1]
    sent = jnp.concatenate(
        [flux_rows.reshape(fluxes * ext_rows, width_atm), sums.reshape(2 * atm_rows, width_atm)],
        axis=0,
    )
    full = summed(sent, ("chan", "lon"))
    flux_full = full[: fluxes * ext_rows].reshape(fluxes, ext_rows, width_atm)
    sums_full = full[fluxes * ext_rows :].reshape(2, atm_rows, width_atm)
    centre = sums_full[0] / CA
    spread = sums_full[1] / CA - centre * centre
    scale = lax.rsqrt(spread + EPSILON)
    normed = (atmos_state - centre) * scale * atmos_gain[:, None, None]
    own = channels // (2 * lat_count)
    halves = (lat_count, 2, own)
    normed = normed.reshape(halves + (atm_rows, width_atm))

    columns = jnp.concatenate([to_ocean[2].astype(jnp.float32), to_ocean[3]], axis=1).T
    columns = jnp.pad(columns, ((0, ocean_rows), (0, 0)))[None]
    state_rows = jnp.concatenate(
        [
            jnp.concatenate([rows_before, ocean_state, rows_after], axis=1),
            jnp.concatenate([mask_above, mask, mask_below], axis=0)[None],
            columns,
        ],
        axis=0,
    )
    state_rim = padded(state_rows, ((("lon", "chan"), 2),), 2)
    surface_rim = jnp.einsum(
        "sc,chw->shw", surface_readout, state_rim[:ocean_channels], precision=EXACT
    )
    row_map = regrid_matrix(
        to_atmos[0], to_atmos[1], lat_place * ocean_rows - 2, ocean_rows + 4, 0
    )
    col_map = regrid_matrix(
        to_atmos[2],
        to_atmos[3],
        col_place * ocean_cols - 2,
        ocean_cols + 4,
        ocean_cols * col_groups,
    )
    atmos_piece = apply_maps(surface_rim, row_map, col_map)
    spread_piece = lax.dynamic_update_slice_in_dim(
        jnp.zeros((fields, atm_rows, width_atm), jnp.float32), atmos_piece, col_place * atm_cols, 2
    )
    surface_atmos = summed(spread_piece, ("chan", "lon"))

    col_tables = state_rim[ocean_channels + 1]
    col_back = regrid_matrix(col_tables[:2].T, col_tables[2:4].T, 0.0, width_atm, 0)
    flux_ocean_rim = jnp.einsum("fhw,kw->fhk", flux_full, col_back, precision=PRECISE)

    mask_rim = state_rim[ocean_channels]
    padded_field = mask_rim * (
        state_rim[:ocean_channels]
        + jnp.einsum("cf,fhw->chw", flux_coupling, flux_ocean_rim, precision=PRECISE)
    )
    update = ocean_mixer(
        depthwise(padded_field, depth_taps[0]), block_gain[0], expand_weight[0], reduce_weight[0]
    )
    widened = mask_rim[1:-1, 1:-1] * (
        padded_field[:, 1:-1, 1:-1] + layer_scale[0][:, None, None] * update
    )
    update = ocean_mixer(
        depthwise(widened, depth_taps[1]), block_gain[1], expand_weight[1], reduce_weight[1]
    )
    ocean_next = mask * (widened[:, 1:-1, 1:-1] + layer_scale[1][:, None, None] * update)

    kernels_first, kernels_rest, normed, ocean_next, surface_atmos = hold(
        (kernels_first, kernels_rest, normed, ocean_next, surface_atmos)
    )
    filtered = spectral_step(normed, kernels_first, kernels_rest)
    by_half = atmos_state.reshape(halves + (atm_rows, width_atm))
    coupling_half = surface_coupling.reshape(halves + (fields, 1, 1))
    forcing = sum(coupling_half[:, :, :, s] * surface_atmos[s] for s in range(fields))
    atmos_next = (by_half + filtered) + forcing
    return (atmos_next.reshape(atmos_state.shape), ocean_next)


def body(
    atmos_state,
    ocean_state,
    land_mask,
    spectral_filter,
    atmos_gain,
    flux_readout,
    surface_coupling,
    surface_readout,
    flux_coupling,
    atmos_row_source,
    atmos_row_weight,
    atmos_col_source,
    atmos_col_weight,
    ocean_row_source,
    ocean_row_weight,
    ocean_col_source,
    ocean_col_weight,
    depth_taps,
    block_gain,
    expand_weight,
    reduce_weight,
    layer_scale,
):
    if channels_divide(atmos_state, spectral_filter, *ocean_state.shape[1:]):
        step = by_channels
    else:
        step = by_frequencies
    return step(
        atmos_state,
        ocean_state,
        land_mask,
        spectral_filter,
        atmos_gain,
        flux_readout,
        surface_coupling,
        surface_readout,
        flux_coupling,
        (atmos_row_source, atmos_row_weight, atmos_col_source, atmos_col_weight),
        (ocean_row_source, ocean_row_weight, ocean_col_source, ocean_col_weight),
        depth_taps,
        block_gain,
        expand_weight,
        reduce_weight,
        layer_scale,
    )


def solution(mesh):
    return jax.shard_map(
        body,
        mesh=mesh,
        in_specs=(
            P(("members", "lon", "chan"), "lat", None),
            P("members", "lat", ("lon", "chan")),
            P("lat", ("lon", "chan")),
            P(None, ("lon", "chan"), "lat", None),
            P(("lon", "chan")),
            P(None, ("lon", "chan")),
            P(("lon", "chan"), None),
            P(),
            P(),
            P("lat", None),
            P("lat", None),
            P(("lon", "chan"), None),
            P(("lon", "chan"), None),
            P("lat", None),
            P("lat", None),
            P(("lon", "chan"), None),
            P(("lon", "chan"), None),
            P(),
            P(),
            P(),
            P(),
            P(),
        ),
        out_specs=(
            P(("members", "lon", "chan"), "lat", None),
            P("members", "lat", ("lon", "chan")),
        ),
        check_vma=False,
    )
```

profile of v0, /device:TPU:0, one launch (start us, length us, event | category | flops | bytes accessed | tf_op | source)
XLA Modules:
  0.0 308.4 jit_solution(16959903923988035258)
XLA Ops:
  0.7 0.7 broadcast_subtract_fusion.1
  1.9 0.7 reduce_sum.90
  2.6 0.7 broadcast_divide_fusion.2
  3.8 3.9 %shard_map.221 = f32[4,2,1,3,96,128]{5,4,3,2,1,0:T(8,128)} custom-call(s32[1]{0:T(128)} %bitcast.member_ref, f32[2,4,2,3,4,96,96]{6,5,4,3,2,1,0:T(8,128)} %bitcast.181), custom_call_target="tpu_custom_call" | custom-call | bytes 3538944 | tf_op jit(solution)/shard_map/pallas_call | solution.py:166
  7.7 0.7 select_add_fusion
  9.0 2.2 fusion.33
  11.2 0.7 copy-done.8
  12.8 1.2 slice_select_fusion
  14.6 0.6 pad_maximum_fusion.3
  15.2 5.1 %collective-permute-start.1 = (f32[9,3,384]{2,0,1:T(8,128)}, f32[9,3,384]{2,0,1:T(8,128)}, u32[]{:S(2)}, u32[]{:S(2)}) collective-permute-start(f32[9,3,384]{2,0,1:T(8,128)} %pad_maximum_fusion.3), channel_id=1, source_target_pairs={{4,0},{8,4},{12,8},{0,12},{5,1},{9,5},{13,9},{1,13},{6,2},{10,6},{... | collective-permute-start | bytes 124424 | tf_op jit(solution)/shard_map/ppermute | solution.py:593
  20.3 2.0 copy.47
  22.3 1.9 fusion.129
  24.1 3.8 %collective-permute-start.5 = (f32[200,2,128]{0,2,1:T(8,128)}, f32[200,2,128]{0,2,1:T(8,128)}, u32[]{:S(2)}, u32[]{:S(2)}) collective-permute-start(f32[200,2,128]{0,2,1:T(8,128)} %get-tuple-element.37), channel_id=1, source_target_pairs={{4,0},{8,4},{12,8},{0,12},{5,1},{9,5},{13,9},{1,13},{6,2},{10,6},{... | collective-permute-start | bytes 614408 | tf_op jit(solution)/shard_map/ppermute | solution.py:591
  28.0 4.3 %all-to-all-start = ((f32[4,2,1,3,96,128]{5,4,3,2,1,0:T(8,128)}), f32[4,2,1,3,96,128]{5,4,3,2,1,0:T(8,128)}, u32[]{:S(2)}, u32[]{:S(2)}) async-start(f32[4,2,1,3,96,128]{5,4,3,2,1,0:T(8,128)} %shard_map.221), calls=%async_computation | async-start | bytes 2359296 | tf_op jit(solution)/shard_map/all_to_all | solution.py:394
  32.3 1.0 fusion.123
  33.3 0.7 broadcast_subtract_fusion
  35.2 0.7 and_select_fusion
  36.4 0.7 reduce_sum.99
  37.1 0.7 broadcast_divide_fusion
  38.4 0.8 fusion.130
  39.8 1.3 fusion.134
  41.2 1.3 fusion.133
  42.5 0.8 reshape.166
  43.9 0.8 pad_maximum_fusion.4
  44.7 0.7 maximum_bitcast_fusion.1
  45.4 0.8 slice.419
  46.2 0.8 fusion.92
  47.0 2.0 collective-permute-start
  49.0 6.4 %shard_map.222 = f32[4,2,2,3,96,128]{5,4,3,2,1,0:T(8,128)} custom-call(s32[1]{0:T(128)} %bitcast.member_ref, f32[2,4,2,3,4,96,96]{6,5,4,3,2,1,0:T(8,128)} %bitcast.182), custom_call_target="tpu_custom_call" | custom-call | bytes 7077888 | tf_op jit(solution)/shard_map/pallas_call | solution.py:166
  55.7 0.7 slice.434
  56.4 3.5 %collective-permute-done = f32[9,3,384]{2,1,0:T(4,128)S(1)} collective-permute-done((f32[9,3,384]{2,1,0:T(4,128)S(1)}, f32[9,3,384]{2,1,0:T(4,128)S(1)}, u32[]{:S(2)}, u32[]{:S(2)}) %collective-permute-start) | collective-permute-done | bytes 41504 | tf_op jit(solution)/shard_map/ppermute | solution.py:592
  60.1 1.4 fusion.93
  61.7 0.9 pad_maximum_fusion.10
  62.6 1.7 collective-permute-start.7
  64.4 0.7 pad_maximum_fusion.1
  65.0 0.7 collective-permute-done.6
  65.8 1.4 pad_maximum_fusion
  67.2 1.0 convolution_bitcast_fusion.1
  68.6 0.9 convolution_bitcast_fusion.2
  69.5 0.9 fusion.79
  70.8 2.2 collective-permute-start.8
  73.0 1.3 maximum_reduce_fusion
  75.1 1.0 fusion.122
  76.6 1.0 dynamic-slice_add_fusion
  77.5 1.5 add.210
  79.0 2.1 collective-permute-start.9
  81.2 1.5 collective-permute-done.3
  83.7 0.8 broadcast_multiply_fusion
  84.6 1.1 fusion.124
  85.7 6.8 %all-to-all-start.1 = ((f32[4,2,2,3,96,128]{5,4,3,2,1,0:T(8,128)}), f32[4,2,2,3,96,128]{5,4,3,2,1,0:T(8,128)}, u32[]{:S(2)}, u32[]{:S(2)}) async-start(f32[4,2,2,3,96,128]{5,4,3,2,1,0:T(8,128)} %shard_map.222), calls=%async_computation.1 | async-start | bytes 4718592 | tf_op jit(solution)/shard_map/all_to_all | solution.py:394
  92.9 2.7 fusion.53
  95.6 2.3 fusion.27
  100.5 0.9 fusion.50
  101.4 2.1 fusion.30
  103.5 2.0 copy.55
  105.5 0.8 slice_multiply_fusion.17
  106.4 3.0 multiply_multiply_fusion.1
  109.4 0.9 add_multiply_fusion.1
  110.3 1.7 add.211
  112.0 34.4 %all-to-all-done.1.rest_ref = f32[4,2,2,3,96,128]{5,4,3,2,1,0:T(8,128)} async-done(((f32[4,2,2,3,96,128]{5,4,3,2,1,0:T(8,128)}), f32[4,2,2,3,96,128]{5,4,3,2,1,0:T(8,128)}, u32[]{:S(2)}, u32[]{:S(2)}) %all-to-all-start.1) | async-done | bytes 2359328 | tf_op jit(solution)/shard_map/all_to_all | solution.py:394
  146.4 1.5 slice_bitcast_fusion.4
  147.9 2.0 copy.60
  149.9 154.2 %shard_map.223 = f32[4,2,12,24,384]{4,3,2,1,0:T(8,128)} custom-call(f32[4,2,12,24,384]{4,3,2,1,0:T(8,128)} %bitcast.183, f32[4,2,1,3,96,128]{5,4,3,2,1,0:T(8,128)} %all-to-all-done.first_ref, f32[4,2,2,3,96,128]{5,4,3,2,1,0:T(8,128)} %all-to-all-done.1.rest_ref), custom_call_target="tpu_custom_call" | custom-call | flops 10192158720 | bytes 10616832 | tf_op jit(solution)/shard_map/pallas_call | solution.py:363
  304.1 4.3 %add_add_fusion = f32[4,2,12,24,384]{4,3,2,1,0:T(8,128)} fusion(f32[4,2,12,24,384]{4,3,2,1,0:T(8,128)S(1)} %bitcast.180, f32[4,2,12,24,384]{4,3,2,1,0:T(8,128)} %shard_map.223, f32[24,384]{1,0:T(8,128)} %get-tuple-element.43, f32[4,2,12]{2,1,0:T(2,128)S(1)} %copy-done.12, f32[24,384]{1,0:T(8,128)} %get-tuple-element.44, f32[4,2,12]{2,1,0:T(2,128)} %get-tuple-element.53, ...), kind=kLoop, calls=%fused_computation.3 | loop fusion | flops 7962624 | bytes 10765824 | tf_op jit(solution)/shard_map/add | solution.py:682
  (126 shorter events, 13.4 us)
Async XLA Ops:
  0.6 83.1 %copy-start = (f32[200,8]{0,1:T(8,128)S(1)}, f32[200,8]{0,1:T(8,128)}, u32[]{:S(2)}) copy-start(f32[200,8]{0,1:T(8,128)} %param.30) | copy-start | bytes 19204
  3.8 5.2 %copy-start.1 = (f32[96,24,384]{2,1,0:T(8,128)S(1)}, f32[96,24,384]{2,1,0:T(8,128)}, u32[]{:S(2)}) copy-start(f32[96,24,384]{2,1,0:T(8,128)} %param.22) | copy-start | bytes 10616836
  3.8 5.2 %copy-start.13 = (f32[8,96]{1,0:T(8,128)S(1)}, f32[8,96]{1,0:T(8,128)}, u32[]{:S(2)}) copy-start(f32[8,96]{1,0:T(8,128)} %param.27) | copy-start | bytes 9220
  9.0 3.8 %copy-start.28 = (pred[3]{0:T(512)(128)(4,1)S(1)}, pred[3]{0:T(512)(128)(4,1)}, u32[]{:S(2)}) copy-start(pred[3]{0:T(512)(128)(4,1)} %constant.73.clone.1) | copy-start | bytes 13
  9.0 5.0 %copy-start.26 = (s32[4,128]{1,0:T(4,128)S(1)}, s32[4,128]{1,0:T(4,128)}, u32[]{:S(2)}) copy-start(s32[4,128]{1,0:T(4,128)} %param.24) | copy-start | bytes 6148
  11.2 0.7 copy-start.8
  12.1 0.6 copy-start.9
  15.2 31.0 %collective-permute-start.1 = (f32[9,3,384]{2,0,1:T(8,128)}, f32[9,3,384]{2,0,1:T(8,128)}, u32[]{:S(2)}, u32[]{:S(2)}) collective-permute-start(f32[9,3,384]{2,0,1:T(8,128)} %pad_maximum_fusion.3), channel_id=1, source_target_pairs={{4,0},{8,4},{12,8},{0,12},{5,1},{9,5},{13,9},{1,13},{6,2},{10,6},{... | collective-permute-start | bytes 124424 | tf_op jit(solution)/shard_map/ppermute | solution.py:593
  24.1 37.5 %collective-permute-start.4 = (f32[200,2,128]{0,2,1:T(8,128)}, f32[200,2,128]{0,2,1:T(8,128)}, u32[]{:S(2)}, u32[]{:S(2)}) collective-permute-start(f32[200,2,128]{0,2,1:T(8,128)} %get-tuple-element.36), channel_id=1, source_target_pairs={{0,4},{4,8},{8,12},{12,0},{1,5},{5,9},{9,13},{13,1},{2,6},{6,10},{... | collective-permute-start | bytes 614408 | tf_op jit(solution)/shard_map/ppermute | solution.py:590
  24.1 37.5 %collective-permute-start.5 = (f32[200,2,128]{0,2,1:T(8,128)}, f32[200,2,128]{0,2,1:T(8,128)}, u32[]{:S(2)}, u32[]{:S(2)}) collective-permute-start(f32[200,2,128]{0,2,1:T(8,128)} %get-tuple-element.37), channel_id=1, source_target_pairs={{4,0},{8,4},{12,8},{0,12},{5,1},{9,5},{13,9},{1,13},{6,2},{10,6},{... | collective-permute-start | bytes 614408 | tf_op jit(solution)/shard_map/ppermute | solution.py:591
  28.0 57.8 %all-to-all-start = ((f32[4,2,1,3,96,128]{5,4,3,2,1,0:T(8,128)}), f32[4,2,1,3,96,128]{5,4,3,2,1,0:T(8,128)}, u32[]{:S(2)}, u32[]{:S(2)}) async-start(f32[4,2,1,3,96,128]{5,4,3,2,1,0:T(8,128)} %shard_map.221), calls=%async_computation | async-start | bytes 2359296 | tf_op jit(solution)/shard_map/all_to_all | solution.py:394
  32.2 1.1 copy-start.23
  32.2 1.1 copy-start.27
  32.3 2.3 copy-start.22
  47.0 12.8 %collective-permute-start = (f32[9,3,384]{2,1,0:T(4,128)S(1)}, f32[9,3,384]{2,1,0:T(4,128)S(1)}, u32[]{:S(2)}, u32[]{:S(2)}) collective-permute-start(f32[9,3,384]{2,1,0:T(4,128)S(1)} %pad_maximum_fusion.5), channel_id=1, source_target_pairs={{0,4},{4,8},{8,12},{12,0},{1,5},{5,9},{9,13},{13,1},{2,6},{6,10},{... | collective-permute-start | bytes 124424 | tf_op jit(solution)/shard_map/ppermute | solution.py:592
  49.0 12.5 %copy-start.11 = (f32[8,3,384]{2,1,0:T(4,128)S(1)}, f32[8,3,384]{2,1,0:T(4,128)}, u32[]{:S(2)}) copy-start(f32[8,3,384]{2,1,0:T(4,128)} %get-tuple-element.48) | copy-start | bytes 110596
  55.4 6.2 %copy-start.5 = (f32[200,4,128]{0,2,1:T(8,128)S(1)}, f32[200,4,128]{0,2,1:T(8,128)}, u32[]{:S(2)}) copy-start(f32[200,4,128]{0,2,1:T(8,128)} %copy.47) | copy-start | bytes 1228804
  62.6 3.2 %collective-permute-start.6 = (f32[202,8,2]{0,2,1:T(2,128)S(1)}, f32[202,8,2]{0,2,1:T(2,128)S(1)}, u32[]{:S(2)}, u32[]{:S(2)}) collective-permute-start(f32[202,8,2]{0,2,1:T(2,128)S(1)} %get-tuple-element.34), channel_id=1, source_target_pairs={{0,1},{1,2},{2,3},{3,0},{4,5},{5,6},{6,7},{7,4},{8,9},{9,10},{10,1... | collective-permute-start | bytes 38792 | tf_op jit(solution)/shard_map/ppermute | solution.py:29
  62.6 3.2 %collective-permute-start.7 = (f32[202,8,2]{0,2,1:T(2,128)S(1)}, f32[202,8,2]{0,2,1:T(2,128)S(1)}, u32[]{:S(2)}, u32[]{:S(2)}) collective-permute-start(f32[202,8,2]{0,2,1:T(2,128)S(1)} %get-tuple-element.35), channel_id=1, source_target_pairs={{1,0},{2,1},{3,2},{0,3},{5,4},{6,5},{7,6},{4,7},{9,8},{10,9},{11,1... | collective-permute-start | bytes 38792 | tf_op jit(solution)/shard_map/ppermute | solution.py:30
  65.0 2.2 copy-start.14
  65.0 10.0 %collective-permute-start.2 = (f32[112,384]{1,0:T(8,128)}, f32[112,384]{1,0:T(8,128)}, u32[]{:S(2)}, u32[]{:S(2)}) collective-permute-start(f32[112,384]{1,0:T(8,128)} %pad_maximum_fusion.1), channel_id=1, source_target_pairs={{0,1},{1,0},{2,3},{3,2},{4,5},{5,4},{6,7},{7,6},{8,9},{9,8},{10,11... | collective-permute-start | bytes 516104 | tf_op jit(solution)/shard_map/ppermute | solution.py:400
  70.8 5.8 %collective-permute-start.8 = (f32[4,24,384]{2,1,0:T(8,128)S(1)}, f32[4,24,384]{2,1,0:T(8,128)}, u32[]{:S(2)}, u32[]{:S(2)}) collective-permute-start(f32[4,24,384]{2,1,0:T(8,128)S(1)} %dynamic_update_slice.5), channel_id=1, source_target_pairs={{0,1},{1,0},{2,3},{3,2},{4,5},{5,4},{6,7},{7,6},{8,9},{9,8},{10,11... | collective-permute-start | bytes 442376 | tf_op jit(solution)/shard_map/ppermute | solution.py:400
  76.0 6.6 %collective-permute-start.3 = (f32[112,384]{1,0:T(8,128)S(1)}, f32[112,384]{1,0:T(8,128)S(1)}, u32[]{:S(2)}, u32[]{:S(2)}) collective-permute-start(f32[112,384]{1,0:T(8,128)S(1)} %fusion.122), channel_id=1, source_target_pairs={{0,2},{2,0},{1,3},{3,1},{4,6},{6,4},{5,7},{7,5},{8,10},{10,8},{9,1... | collective-permute-start | bytes 516104 | tf_op jit(solution)/shard_map/ppermute | solution.py:400
  79.0 31.3 %collective-permute-start.9 = (f32[4,24,384]{2,1,0:T(8,128)}, f32[4,24,384]{2,1,0:T(8,128)}, u32[]{:S(2)}, u32[]{:S(2)}) collective-permute-start(f32[4,24,384]{2,1,0:T(8,128)} %add.210), channel_id=1, source_target_pairs={{0,2},{2,0},{1,3},{3,1},{4,6},{6,4},{5,7},{7,5},{8,10},{10,8},{9,1... | collective-permute-start | bytes 442376 | tf_op jit(solution)/shard_map/ppermute | solution.py:400
  82.7 0.7 copy-start.10
  82.7 1.8 copy-start.15
  82.7 1.8 copy-start.16
  82.7 1.8 copy-start.17
  82.7 1.8 copy-start.18
  82.7 1.8 copy-start.19
  85.7 6.8 %copy-start.25 = (f32[1,200]{1,0:T(1,128)S(1)}, f32[1,200]{1,0:T(1,128)}, u32[]{:S(2)}) copy-start(f32[1,200]{1,0:T(1,128)} %get-tuple-element.80) | copy-start | bytes 2404
  85.7 60.7 %all-to-all-start.1 = ((f32[4,2,2,3,96,128]{5,4,3,2,1,0:T(8,128)}), f32[4,2,2,3,96,128]{5,4,3,2,1,0:T(8,128)}, u32[]{:S(2)}, u32[]{:S(2)}) async-start(f32[4,2,2,3,96,128]{5,4,3,2,1,0:T(8,128)} %shard_map.222), calls=%async_computation.1 | async-start | bytes 4718592 | tf_op jit(solution)/shard_map/all_to_all | solution.py:394
  92.9 2.7 copy-start.29
  97.9 0.7 copy-start.21
  98.8 0.9 copy-start.3
  98.8 0.9 copy-start.20
  98.8 1.7 copy-start.7
  99.9 1.5 copy-start.30
  101.4 4.9 %copy-start.2 = (f32[96,24,384]{2,1,0:T(8,128)S(1)}, f32[96,24,384]{2,1,0:T(8,128)}, u32[]{:S(2)}) copy-start(f32[96,24,384]{2,1,0:T(8,128)} %param.22) | copy-start | bytes 10616836
  106.3 3.0 copy-start.4
  106.3 3.0 copy-start.6
  106.4 3.0 copy-start.24
  149.9 154.2 %copy-start.12 = (f32[4,2,12]{2,1,0:T(2,128)S(1)}, f32[4,2,12]{2,1,0:T(2,128)}, u32[]{:S(2)}) copy-start(f32[4,2,12]{2,1,0:T(2,128)} %get-tuple-element.52) | copy-start | bytes 1156
where the time goes:
time: 310 us; the launch traced here: 308 us
  Pallas kernels  164 us (53%)
  waiting for transfers between devices  40.2 us (13%)
  other arithmetic  31.7 us (10%)
  starting transfers between devices  28.6 us (9%)
  local copies, waits for them, and re-layouts  27.9 us (9%)
  matrix products  14.4 us (5%)
    pallas_call x1, Pallas kernels, spectral_step(): pl.pallas_call(spectral_kernel, out_shape=jax.ShapeDtypeStruct(normed.sha...  154 us
    all_to_all x2, waiting for transfers between devices, exchanged(): return lax.all_to_all(x, 'lat', split_axis=0, concat_axis=0, tiled=True)  34.4 us
    all_to_all x2, starting transfers between devices, exchanged(): return lax.all_to_all(x, 'lat', split_axis=0, concat_axis=0, tiled=True)  11.1 us
    pallas_call x2, Pallas kernels, pack_filter(): pl.pallas_call(pack_kernel, out_shape=jax.ShapeDtypeStruct((lat_count, pa...  10.3 us
  transfers between devices with their start and end apart: 12, of which 4 were waited for; matrix products, arithmetic and copies ran while one was open for 17% of the time, Pallas kernels for 2%

commit v1 on v0

--- a/solution.py
+++ b/solution.py
@@ -17,6 +17,7 @@
 LANES = 128
 PACK = 4
 TABLE_ROWS = 16
+RIM = 9
 
 
 def padded(x, sides, width):
@@ -229,9 +230,40 @@
         out_ref[:, j] = own.reshape(blocks, block_rows, width)
 
 
+def ocean_block(which, source, mask_ref, taps_ref, gain_ref, scale_ref, weights, span, store):
+    channels = source.shape[2]
+    columns = span.stop - span.start
+    expand_hi, expand_lo, reduce_hi, reduce_lo = weights
+
+    def one_row(index, carry):
+        row = index + 1 + which
+        conv = jnp.zeros((columns, channels), jnp.float32)
+        for row_off in range(3):
+            for col_off in range(3):
+                tap = 3 * row_off + col_off
+                begin = span.start + col_off - 1
+                conv = conv + taps_ref[which, tap : tap + 1, :] * (
+                    source[row + row_off - 1, begin : begin + columns, :]
+                )
+        centre = jnp.sum(conv, axis=1, keepdims=True) / channels
+        spread = jnp.sum(conv * conv, axis=1, keepdims=True) / channels - centre * centre
+        normed = (conv - centre) * lax.rsqrt(spread + EPSILON) * gain_ref[which]
+        hidden = jax.nn.gelu(product(split_value(normed), (expand_hi[...], expand_lo[...])))
+        update = product(split_value(hidden), (reduce_hi[...], reduce_lo[...]))
+        store(
+            row,
+            mask_ref[row, span, :] * (source[row, span, :] + scale_ref[which] * update),
+        )
+        return carry
+
+    lax.fori_loop(0, source.shape[0] - 2 - 2 * which, one_row, 0)
+
+
 def spectral_kernel(
-    normed_ref, first_ref, rest_ref, out_ref,
+    normed_ref, first_ref, rest_ref, expand_from, reduce_from,
+    field_ref, mask_ref, taps_ref, gain_ref, scale_ref, out_ref, ocean_ref,
     kernels_ref, arrived_ref, back_ref, wide_ref, w_hi, w_lo, f_hi, f_lo, b_hi, b_lo,
+    second_ref, expand_ref, reduce_ref, expand_hi, expand_lo, reduce_hi, reduce_lo, weight_sem,
     go_send, go_recv, go_local, come_send, come_recv, come_local, swap_send, swap_recv, own_sem,
 ):
     count = normed_ref.shape[0]
@@ -313,7 +345,31 @@
             own_filter(step).start()
             swapped(step).start()
 
+    fetches = [
+        pltpu.make_async_copy(expand_from, expand_ref, weight_sem.at[0]),
+        pltpu.make_async_copy(reduce_from, reduce_ref, weight_sem.at[1]),
+    ]
+    for fetch in fetches:
+        fetch.start()
     fill_tables(w_hi, w_lo, f_hi, f_lo, b_hi, b_lo)
+    for fetch in fetches:
+        fetch.wait()
+
+    def keep_second(row, values):
+        second_ref[row, 8 : 8 + values.shape[0], :] = values
+
+    def keep_ocean(row, values):
+        ocean_ref[row - 2] = values
+
+    wide_columns = field_ref.shape[1]
+    spans = (slice(8, wide_columns - 8), slice(RIM, RIM + ocean_ref.shape[1]))
+    for which, source, store in ((0, field_ref, keep_second), (1, second_ref, keep_ocean)):
+        expand_hi[...], expand_lo[...] = split_value(expand_ref[which])
+        reduce_hi[...], reduce_lo[...] = split_value(reduce_ref[which])
+        ocean_block(
+            which, source, mask_ref, taps_ref, gain_ref, scale_ref,
+            (expand_hi, expand_lo, reduce_hi, reduce_lo), spans[which], store,
+        )
 
     def one_step(step, carry):
         staying(step).wait()
@@ -352,25 +408,38 @@
             coming(step, k, peer).wait()
 
 
-def spectral_step(normed, first, rest):
+def spectral_step(normed, first, rest, expand, reduce_w, field, mask, taps, gain, scale):
     lat_count, halves, _, rows, width = normed.shape
     parts, groups = first.shape[1], first.shape[2] + rest.shape[2]
     height = lat_count * rows
     steps = halves * groups
+    rows_out, cols_out = field.shape[0] - 4, field.shape[1] - 24
     anywhere = pl.BlockSpec(memory_space=pl.ANY)
+    inside = pl.BlockSpec(memory_space=pltpu.VMEM)
     dma = pltpu.SemaphoreType.DMA
     tables = [(width, 2 * width)] * 2 + [(2 * height, 2 * height)] * 4
     return pl.pallas_call(
         spectral_kernel,
-        out_shape=jax.ShapeDtypeStruct(normed.shape, jnp.float32),
-        in_specs=[anywhere] * 3,
-        out_specs=anywhere,
+        out_shape=(
+            jax.ShapeDtypeStruct(normed.shape, jnp.float32),
+            jax.ShapeDtypeStruct((rows_out, cols_out, field.shape[2]), jnp.float32),
+        ),
+        in_specs=[anywhere] * 5 + [inside] * 5,
+        out_specs=(anywhere, inside),
         scratch_shapes=[
             pltpu.VMEM((steps, lat_count, parts) + first.shape[3:], jnp.float32),
             pltpu.VMEM((steps, lat_count, PACK, rows, width), jnp.float32),
             pltpu.VMEM((steps, lat_count, PACK, rows, width), jnp.float32),
             pltpu.VMEM((PACK * height, 2 * width), jnp.float32),
             *(pltpu.VMEM(shape, jnp.bfloat16) for shape in tables),
+            pltpu.VMEM(field.shape, jnp.float32),
+            pltpu.VMEM(expand.shape, jnp.float32),
+            pltpu.VMEM(reduce_w.shape, jnp.float32),
+            pltpu.VMEM(expand.shape[1:], jnp.bfloat16),
+            pltpu.VMEM(expand.shape[1:], jnp.bfloat16),
+            pltpu.VMEM(reduce_w.shape[1:], jnp.bfloat16),
+            pltpu.VMEM(reduce_w.shape[1:], jnp.bfloat16),
+            dma((2,)),
             dma((steps, lat_count - 1)),
             dma((steps, lat_count - 1)),
             dma((steps,)),
@@ -387,7 +456,7 @@
             transcendentals=0,
             bytes_accessed=8 * normed.size + 4 * (first.size + rest.size),
         ),
-    )(normed, first, rest)
+    )(normed, first, rest, expand, reduce_w, field, mask, taps, gain, scale)
 
 
 def exchanged(x):
@@ -417,6 +486,7 @@
         and (lax.axis_size("lat") * rows) % TABLE_ROWS == 0
         and width % TABLE_ROWS == 0
         and channels > unit
+        and ocean_cols % 8 == 0
         and width >= ocean_cols
         and rows % ocean_rows == 0
         and ocean_rows >= 4
@@ -636,6 +706,7 @@
     surface_rim = jnp.einsum(
         "sc,chw->shw", surface_readout, state_rim[:ocean_channels], precision=EXACT
     )
+    to_atmos, state_rim = hold((to_atmos, state_rim))
     row_map = regrid_matrix(
         to_atmos[0], to_atmos[1], lat_place * ocean_rows - 2, ocean_rows + 4, 0
     )
@@ -661,21 +732,18 @@
         state_rim[:ocean_channels]
         + jnp.einsum("cf,fhw->chw", flux_coupling, flux_ocean_rim, precision=PRECISE)
     )
-    update = ocean_mixer(
-        depthwise(padded_field, depth_taps[0]), block_gain[0], expand_weight[0], reduce_weight[0]
-    )
-    widened = mask_rim[1:-1, 1:-1] * (
-        padded_field[:, 1:-1, 1:-1] + layer_scale[0][:, None, None] * update
-    )
-    update = ocean_mixer(
-        depthwise(widened, depth_taps[1]), block_gain[1], expand_weight[1], reduce_weight[1]
-    )
-    ocean_next = mask * (widened[:, 1:-1, 1:-1] + layer_scale[1][:, None, None] * update)
-
-    kernels_first, kernels_rest, normed, ocean_next, surface_atmos = hold(
-        (kernels_first, kernels_rest, normed, ocean_next, surface_atmos)
-    )
-    filtered = spectral_step(normed, kernels_first, kernels_rest)
+    aside = ((0, 0), (RIM - 2, 24 - RIM - 2))
+    field = jnp.pad(jnp.transpose(padded_field, (1, 2, 0)), aside + ((0, 0),))
+    mask_field = jnp.pad(mask_rim, aside)[:, :, None]
+    small = (jnp.transpose(depth_taps, (0, 2, 1)), block_gain[:, None], layer_scale[:, None])
+
+    kernels_first, kernels_rest, normed, field, surface_atmos = hold(
+        (kernels_first, kernels_rest, normed, field, surface_atmos)
+    )
+    filtered, ocean_rows_next = spectral_step(
+        normed, kernels_first, kernels_rest, expand_weight, reduce_weight, field, mask_field, *small
+    )
+    ocean_next = jnp.transpose(ocean_rows_next, (2, 0, 1))
     by_half = atmos_state.reshape(halves + (atm_rows, width_atm))
     coupling_half = surface_coupling.reshape(halves + (fields, 1, 1))
     forcing = sum(coupling_half[:, :, :, s] * surface_atmos[s] for s in range(fields))

time: 310 us -> 312 us (level)
  local copies, waits for them, and re-layouts: 27.9 us -> 43.2 us
  waiting for transfers between devices: 40.2 us -> 25 us
  other arithmetic: 31.7 us -> 37.4 us
  matrix products: 14.4 us -> 9.69 us
    all_to_all x2, waiting for transfers between devices: 34.4 us -> 24.1 us  [exchanged(): return lax.all_to_all(x, 'lat', split_axis=0, concat_axis=0, tiled=True)]
    dot_general x4 -> x0, matrix products: 7.99 us -> none  [the longest x2 4.38 us: ocean_mixer(): update = jnp.einsum('dc,dp->cp', reduce_w, hidden, precision=PRECISE)]
    broadcast_in_dim x0 -> x4, local copies, waits for them, and re-layouts: none -> 5.05 us  [the longest x2 2.5 us: by_channels(): mask_field = jnp.pad(mask_rim, aside)[:, :, None]]
    slice x6 -> x0, local copies, waits for them, and re-layouts: 4.17 us -> none  [the longest x1 1.33 us: by_channels(): block_gain[1]]
    ppermute x1, waiting for transfers between devices: 3.46 us -> 0.01 us  [by_channels(): from_above = lax.ppermute(to_below, 'lat', up)]
    unnamed x63 -> x27, local copies, waits for them, and re-layouts: 5.12 us -> 7.73 us
  transfers between devices with their start and end apart: 12 -> 12, of which waited for: 4 -> 2; matrix products, arithmetic and copies ran while one was open for 17% -> 23% of each run, Pallas kernels for 2% -> 2%
where the time goes in v1:
time: 312 us; the launch traced here: 309 us
  Pallas kernels  167 us (54%)
  local copies, waits for them, and re-layouts  43.2 us (14%)
  other arithmetic  37.4 us (12%)
  starting transfers between devices  26.2 us (8%)
  waiting for transfers between devices  25 us (8%)
  matrix products  9.69 us (3%)
    pallas_call x1, Pallas kernels, spectral_step(): pl.pallas_call(spectral_kernel, out_shape=(jax.ShapeDtypeStruct(normed.sh...  157 us
    all_to_all x2, waiting for transfers between devices, exchanged(): return lax.all_to_all(x, 'lat', split_axis=0, concat_axis=0, tiled=True)  24.1 us
    pallas_call x2, Pallas kernels, pack_filter(): pl.pallas_call(pack_kernel, out_shape=jax.ShapeDtypeStruct((lat_count, pa...  10.3 us
    all_to_all x2, starting transfers between devices, exchanged(): return lax.all_to_all(x, 'lat', split_axis=0, concat_axis=0, tiled=True)  8.97 us
    unnamed x27, local copies, waits for them, and re-layouts  7.73 us
  transfers between devices with their start and end apart: 12, of which 2 were waited for; matrix products, arithmetic and copies ran while one was open for 23% of the time, Pallas kernels for 2%

profile of v1, /device:TPU:0, one launch (start us, length us, event | category | flops | bytes accessed | tf_op | source)
XLA Modules:
  0.0 309.5 jit_solution(13267439928268876326)
XLA Ops:
  1.9 0.7 reduce_sum.54
  3.9 3.9 %shard_map.221 = f32[4,2,1,3,96,128]{5,4,3,2,1,0:T(8,128)} custom-call(s32[1]{0:T(128)} %bitcast.member_ref, f32[2,4,2,3,4,96,96]{6,5,4,3,2,1,0:T(8,128)} %bitcast.124), custom_call_target="tpu_custom_call" | custom-call | bytes 3538944 | tf_op jit(solution)/shard_map/pallas_call | solution.py:167
  7.8 0.8 select_add_fusion
  9.1 2.2 fusion.5
  11.3 0.7 copy-done.3
  12.9 1.2 slice_select_fusion
  15.4 5.1 %collective-permute-start.1 = (f32[9,3,384]{2,0,1:T(8,128)}, f32[9,3,384]{2,0,1:T(8,128)}, u32[]{:S(2)}, u32[]{:S(2)}) collective-permute-start(f32[9,3,384]{2,0,1:T(8,128)} %pad_maximum_fusion.2), channel_id=1, source_target_pairs={{4,0},{8,4},{12,8},{0,12},{5,1},{9,5},{13,9},{1,13},{6,2},{10,6},{... | collective-permute-start | bytes 124424 | tf_op jit(solution)/shard_map/ppermute | solution.py:663
  20.5 2.0 copy.74
  22.5 1.9 fusion.61
  24.4 3.8 %collective-permute-start.5 = (f32[200,2,128]{0,2,1:T(8,128)}, f32[200,2,128]{0,2,1:T(8,128)}, u32[]{:S(2)}, u32[]{:S(2)}) collective-permute-start(f32[200,2,128]{0,2,1:T(8,128)} %get-tuple-element.48), channel_id=1, source_target_pairs={{4,0},{8,4},{12,8},{0,12},{5,1},{9,5},{13,9},{1,13},{6,2},{10,6},{... | collective-permute-start | bytes 614408 | tf_op jit(solution)/shard_map/ppermute | solution.py:661
  28.2 4.3 %all-to-all-start = ((f32[4,2,1,3,96,128]{5,4,3,2,1,0:T(8,128)}), f32[4,2,1,3,96,128]{5,4,3,2,1,0:T(8,128)}, u32[]{:S(2)}, u32[]{:S(2)}) async-start(f32[4,2,1,3,96,128]{5,4,3,2,1,0:T(8,128)} %shard_map.221), calls=%async_computation | async-start | bytes 2359296 | tf_op jit(solution)/shard_map/all_to_all | solution.py:463
  32.5 1.1 fusion.60
  34.2 1.3 convert_element_type.12
  35.4 1.4 reshape.62
  36.8 1.3 slice_bitcast_fusion.8
  38.1 1.4 pad_maximum_fusion.3
  39.5 0.7 maximum_bitcast_fusion.1
  40.2 0.8 slice.232
  41.0 1.4 fusion.39
  43.1 2.0 collective-permute-start
  45.1 6.4 %shard_map.222 = f32[4,2,2,3,96,128]{5,4,3,2,1,0:T(8,128)} custom-call(s32[1]{0:T(128)} %bitcast.member_ref, f32[2,4,2,3,4,96,96]{6,5,4,3,2,1,0:T(8,128)} %bitcast.125), custom_call_target="tpu_custom_call" | custom-call | bytes 7077888 | tf_op jit(solution)/shard_map/pallas_call | solution.py:167
  51.5 1.1 copy.78
  52.5 3.0 copy.82.reduce_from
  55.6 1.3 copy.100
  56.9 1.3 broadcast_in_dim.42.gain_ref
  58.2 1.3 broadcast_in_dim.43.scale_ref
  59.5 1.3 copy.72
  60.8 1.3 copy.73
  62.1 0.7 slice.247
  63.4 1.0 copy.77
  64.5 1.4 slice.234
  65.9 2.0 fusion.40
  67.9 1.6 concatenate.37
  69.5 1.0 pad_maximum_fusion.9
  70.6 1.7 collective-permute-start.7
  72.3 1.6 pad_maximum_fusion.1
  73.9 2.9 pad_maximum_fusion
  76.8 0.7 reduce_sum.59
  77.5 0.7 reduce_sum.58
  82.6 2.9 fusion.10
  85.6 4.7 %all-to-all-start.1 = ((f32[4,2,2,3,96,128]{5,4,3,2,1,0:T(8,128)}), f32[4,2,2,3,96,128]{5,4,3,2,1,0:T(8,128)}, u32[]{:S(2)}, u32[]{:S(2)}) async-start(f32[4,2,2,3,96,128]{5,4,3,2,1,0:T(8,128)} %shard_map.222), calls=%async_computation.1 | async-start | bytes 4718592 | tf_op jit(solution)/shard_map/all_to_all | solution.py:463
  90.2 1.0 convolution_bitcast_fusion.1
  91.3 1.5 fusion.25
  93.4 1.5 dynamic_update_slice.5
  94.9 2.0 collective-permute-start.8
  96.9 1.6 slice_reduce_fusion
  99.2 1.8 copy.83.mask_ref
  101.0 1.4 slice_reduce_fusion.1
  103.6 1.7 fusion.59
  105.5 1.6 dynamic-slice_add_fusion
  107.2 1.5 add.94
  108.7 2.3 collective-permute-start.9
  111.0 0.9 collective-permute-done.3
  111.9 1.0 add.84
  112.9 1.1 fusion.14
  114.0 3.0 multiply_multiply_fusion
  117.0 0.8 fusion.4
  117.8 1.3 pad.23.field_ref
  119.1 1.6 add.95
  120.7 24.1 %all-to-all-done.1.rest_ref = f32[4,2,2,3,96,128]{5,4,3,2,1,0:T(8,128)} async-done(((f32[4,2,2,3,96,128]{5,4,3,2,1,0:T(8,128)}), f32[4,2,2,3,96,128]{5,4,3,2,1,0:T(8,128)}, u32[]{:S(2)}, u32[]{:S(2)}) %all-to-all-start.1) | async-done | bytes 2359328 | tf_op jit(solution)/shard_map/all_to_all | solution.py:463
  144.8 1.5 slice_bitcast_fusion.4
  146.3 156.9 %shard_map.223 = (f32[4,2,12,24,384]{4,3,2,1,0:T(8,128)}, f32[4,128,200]{2,1,0:T(8,128)}) custom-call(f32[4,2,12,24,384]{4,3,2,1,0:T(8,128)} %bitcast.126, f32[4,2,1,3,96,128]{5,4,3,2,1,0:T(8,128)} %all-to-all-done.first_ref, f32[4,2,2,3,96,128]{5,4,3,2,1,0:T(8,128)} %all-to-all-done.1.rest_ref, f32[2,200,800]{2,1,0:T(8,128)} %expand_from.1, ...), custom_call_target="tpu_custom_call" | custom-call | flops 10192158720 | bytes 10616832 | tf_op jit(solution)/shard_map/pallas_call | solution.py:421
  303.2 2.0 copy.88
  305.2 4.3 %add_add_fusion = f32[4,2,12,24,384]{4,3,2,1,0:T(8,128)} fusion(f32[4,2,12,24,384]{4,3,2,1,0:T(8,128)S(1)} %bitcast.123, f32[4,2,12,24,384]{4,3,2,1,0:T(8,128)} %get-tuple-element.29, f32[24,384]{1,0:T(8,128)} %get-tuple-element.54, f32[4,2,12]{2,1,0:T(2,128)S(1)} %copy-done.8, f32[24,384]{1,0:T(8,128)} %get-tuple-element.55, ...), kind=kLoop, calls=%fused_computation.2 | loop fusion | flops 7962624 | bytes 10765824 | tf_op jit(solution)/shard_map/add | solution.py:750
  (70 shorter events, 14.6 us)
Async XLA Ops:
  0.6 116.4 %copy-start = (f32[200,8]{0,1:T(8,128)S(1)}, f32[200,8]{0,1:T(8,128)}, u32[]{:S(2)}) copy-start(f32[200,8]{0,1:T(8,128)} %param.30) | copy-start | bytes 19204
  3.9 5.2 %copy-start.1 = (f32[96,24,384]{2,1,0:T(8,128)S(1)}, f32[96,24,384]{2,1,0:T(8,128)}, u32[]{:S(2)}) copy-start(f32[96,24,384]{2,1,0:T(8,128)} %param.22) | copy-start | bytes 10616836
  3.9 5.2 %copy-start.9 = (f32[8,96]{1,0:T(8,128)S(1)}, f32[8,96]{1,0:T(8,128)}, u32[]{:S(2)}) copy-start(f32[8,96]{1,0:T(8,128)} %param.27) | copy-start | bytes 9220
  7.8 5.1 %copy-start.11 = (pred[3]{0:T(512)(128)(4,1)S(1)}, pred[3]{0:T(512)(128)(4,1)}, u32[]{:S(2)}) copy-start(pred[3]{0:T(512)(128)(4,1)} %constant.57.clone.1) | copy-start | bytes 13
  7.8 6.3 %copy-start.10 = (s32[4,128]{1,0:T(4,128)S(1)}, s32[4,128]{1,0:T(4,128)}, u32[]{:S(2)}) copy-start(s32[4,128]{1,0:T(4,128)} %param.24) | copy-start | bytes 6148
  11.3 0.7 copy-start.3
  12.3 0.6 copy-start.4
  14.1 0.6 copy-start.5
  15.4 25.6 %collective-permute-start.1 = (f32[9,3,384]{2,0,1:T(8,128)}, f32[9,3,384]{2,0,1:T(8,128)}, u32[]{:S(2)}, u32[]{:S(2)}) collective-permute-start(f32[9,3,384]{2,0,1:T(8,128)} %pad_maximum_fusion.2), channel_id=1, source_target_pairs={{4,0},{8,4},{12,8},{0,12},{5,1},{9,5},{13,9},{1,13},{6,2},{10,6},{... | collective-permute-start | bytes 124424 | tf_op jit(solution)/shard_map/ppermute | solution.py:663
  24.3 45.2 %collective-permute-start.4 = (f32[200,2,128]{0,2,1:T(8,128)}, f32[200,2,128]{0,2,1:T(8,128)}, u32[]{:S(2)}, u32[]{:S(2)}) collective-permute-start(f32[200,2,128]{0,2,1:T(8,128)} %get-tuple-element.47), channel_id=1, source_target_pairs={{0,4},{4,8},{8,12},{12,0},{1,5},{5,9},{9,13},{13,1},{2,6},{6,10},{... | collective-permute-start | bytes 614408 | tf_op jit(solution)/shard_map/ppermute | solution.py:660
  24.4 45.2 %collective-permute-start.5 = (f32[200,2,128]{0,2,1:T(8,128)}, f32[200,2,128]{0,2,1:T(8,128)}, u32[]{:S(2)}, u32[]{:S(2)}) collective-permute-start(f32[200,2,128]{0,2,1:T(8,128)} %get-tuple-element.48), channel_id=1, source_target_pairs={{4,0},{8,4},{12,8},{0,12},{5,1},{9,5},{13,9},{1,13},{6,2},{10,6},{... | collective-permute-start | bytes 614408 | tf_op jit(solution)/shard_map/ppermute | solution.py:661
  28.2 57.4 %all-to-all-start = ((f32[4,2,1,3,96,128]{5,4,3,2,1,0:T(8,128)}), f32[4,2,1,3,96,128]{5,4,3,2,1,0:T(8,128)}, u32[]{:S(2)}, u32[]{:S(2)}) async-start(f32[4,2,1,3,96,128]{5,4,3,2,1,0:T(8,128)} %shard_map.221), calls=%async_computation | async-start | bytes 2359296 | tf_op jit(solution)/shard_map/all_to_all | solution.py:463
  43.1 19.7 %collective-permute-start = (f32[9,3,384]{2,1,0:T(4,128)}, f32[9,3,384]{2,1,0:T(4,128)}, u32[]{:S(2)}, u32[]{:S(2)}) collective-permute-start(f32[9,3,384]{2,1,0:T(4,128)} %pad_maximum_fusion.4), channel_id=1, source_target_pairs={{0,4},{4,8},{8,12},{12,0},{1,5},{5,9},{9,13},{13,1},{2,6},{6,10},{... | collective-permute-start | bytes 124424 | tf_op jit(solution)/shard_map/ppermute | solution.py:662
  51.5 12.0 %copy-start.6 = (f32[4,128]{1,0:T(4,128)S(1)}, f32[4,128]{1,0:T(4,128)}, u32[]{:S(2)}) copy-start(f32[4,128]{1,0:T(4,128)} %copy-done.5) | copy-start | bytes 6148
  70.5 3.4 %collective-permute-start.6 = (f32[202,8,2]{0,2,1:T(2,128)S(1)}, f32[202,8,2]{0,2,1:T(2,128)S(1)}, u32[]{:S(2)}, u32[]{:S(2)}) collective-permute-start(f32[202,8,2]{0,2,1:T(2,128)S(1)} %get-tuple-element.45), channel_id=1, source_target_pairs={{0,1},{1,2},{2,3},{3,0},{4,5},{5,6},{6,7},{7,4},{8,9},{9,10},{10,1... | collective-permute-start | bytes 38792 | tf_op jit(solution)/shard_map/ppermute | solution.py:30
  70.6 3.4 %collective-permute-start.7 = (f32[202,8,2]{0,2,1:T(2,128)S(1)}, f32[202,8,2]{0,2,1:T(2,128)S(1)}, u32[]{:S(2)}, u32[]{:S(2)}) collective-permute-start(f32[202,8,2]{0,2,1:T(2,128)S(1)} %get-tuple-element.46), channel_id=1, source_target_pairs={{1,0},{2,1},{3,2},{0,3},{5,4},{6,5},{7,6},{4,7},{9,8},{10,9},{11,1... | collective-permute-start | bytes 38792 | tf_op jit(solution)/shard_map/ppermute | solution.py:31
  73.9 29.7 %collective-permute-start.2 = (f32[112,384]{1,0:T(8,128)}, f32[112,384]{1,0:T(8,128)}, u32[]{:S(2)}, u32[]{:S(2)}) collective-permute-start(f32[112,384]{1,0:T(8,128)} %pad_maximum_fusion.1), channel_id=1, source_target_pairs={{0,1},{1,0},{2,3},{3,2},{4,5},{5,4},{6,7},{7,6},{8,9},{9,8},{10,11... | collective-permute-start | bytes 516104 | tf_op jit(solution)/shard_map/ppermute | solution.py:469
  85.6 59.2 %all-to-all-start.1 = ((f32[4,2,2,3,96,128]{5,4,3,2,1,0:T(8,128)}), f32[4,2,2,3,96,128]{5,4,3,2,1,0:T(8,128)}, u32[]{:S(2)}, u32[]{:S(2)}) async-start(f32[4,2,2,3,96,128]{5,4,3,2,1,0:T(8,128)} %shard_map.222), calls=%async_computation.1 | async-start | bytes 4718592 | tf_op jit(solution)/shard_map/all_to_all | solution.py:463
  94.9 10.6 %collective-permute-start.8 = (f32[4,24,384]{2,1,0:T(8,128)}, f32[4,24,384]{2,1,0:T(8,128)}, u32[]{:S(2)}, u32[]{:S(2)}) collective-permute-start(f32[4,24,384]{2,1,0:T(8,128)} %dynamic_update_slice.5), channel_id=1, source_target_pairs={{0,1},{1,0},{2,3},{3,2},{4,5},{5,4},{6,7},{7,6},{8,9},{9,8},{10,11... | collective-permute-start | bytes 442376 | tf_op jit(solution)/shard_map/ppermute | solution.py:469
  105.3 6.6 %collective-permute-start.3 = (f32[112,384]{1,0:T(8,128)}, f32[112,384]{1,0:T(8,128)}, u32[]{:S(2)}, u32[]{:S(2)}) collective-permute-start(f32[112,384]{1,0:T(8,128)} %fusion.59), channel_id=1, source_target_pairs={{0,2},{2,0},{1,3},{3,1},{4,6},{6,4},{5,7},{7,5},{8,10},{10,8},{9,1... | collective-permute-start | bytes 516104 | tf_op jit(solution)/shard_map/ppermute | solution.py:469
  108.7 10.4 %collective-permute-start.9 = (f32[4,24,384]{2,1,0:T(8,128)}, f32[4,24,384]{2,1,0:T(8,128)S(1)}, u32[]{:S(2)}, u32[]{:S(2)}) collective-permute-start(f32[4,24,384]{2,1,0:T(8,128)} %add.94), channel_id=1, source_target_pairs={{0,2},{2,0},{1,3},{3,1},{4,6},{6,4},{5,7},{7,5},{8,10},{10,8},{9,1... | collective-permute-start | bytes 442376 | tf_op jit(solution)/shard_map/ppermute | solution.py:469
  114.0 3.0 copy-start.2
  146.3 158.9 %copy-start.7 = (f32[4,2,12]{2,1,0:T(2,128)S(1)}, f32[4,2,12]{2,1,0:T(2,128)}, u32[]{:S(2)}) copy-start(f32[4,2,12]{2,1,0:T(2,128)} %get-tuple-element.60) | copy-start | bytes 1156
  146.3 158.9 %copy-start.8 = (f32[4,2,12]{2,1,0:T(2,128)S(1)}, f32[4,2,12]{2,1,0:T(2,128)}, u32[]{:S(2)}) copy-start(f32[4,2,12]{2,1,0:T(2,128)} %get-tuple-element.61) | copy-start | bytes 1156

commit v2 on v1

--- a/solution.py
+++ b/solution.py
@@ -18,6 +18,8 @@
 PACK = 4
 TABLE_ROWS = 16
 RIM = 9
+PACK_VMEM = 4 << 20
+STEP_VMEM = 36 << 20
 
 
 def padded(x, sides, width):
@@ -144,6 +146,15 @@
 
 def product(left, right):
     dot = functools.partial(jnp.dot, preferred_element_type=jnp.float32)
+    return dot(left[0], right[0]) + (dot(left[0], right[1]) + dot(left[1], right[0]))
+
+
+def product_transposed(left, right):
+    dot = functools.partial(
+        lax.dot_general,
+        dimension_numbers=(((1,), (1,)), ((), ())),
+        preferred_element_type=jnp.float32,
+    )
     return dot(left[0], right[0]) + (dot(left[0], right[1]) + dot(left[1], right[0]))
 
 
@@ -182,6 +193,7 @@
                 (1, parts, 1, PACK - 1, freqs, LANES), lambda i, g, m: (i, 0, g, 0, 0, 0)
             ),
         ),
+        compiler_params=pltpu.CompilerParams(vmem_limit_bytes=PACK_VMEM),
         cost_estimate=pl.CostEstimate(
             flops=0,
             transcendentals=0,
@@ -247,12 +259,12 @@
                 )
         centre = jnp.sum(conv, axis=1, keepdims=True) / channels
         spread = jnp.sum(conv * conv, axis=1, keepdims=True) / channels - centre * centre
-        normed = (conv - centre) * lax.rsqrt(spread + EPSILON) * gain_ref[which]
+        normed = (conv - centre) * lax.rsqrt(spread + EPSILON) * gain_ref[which : which + 1, :]
         hidden = jax.nn.gelu(product(split_value(normed), (expand_hi[...], expand_lo[...])))
-        update = product(split_value(hidden), (reduce_hi[...], reduce_lo[...]))
+        update = product_transposed(split_value(hidden), (reduce_hi[...], reduce_lo[...]))
         store(
             row,
-            mask_ref[row, span, :] * (source[row, span, :] + scale_ref[which] * update),
+            mask_ref[row, span, :] * (source[row, span, :] + scale_ref[which : which + 1, :] * update),
         )
         return carry
 
@@ -450,7 +462,9 @@
             dma((groups,)),
             dma((groups,)),
         ],
-        compiler_params=pltpu.CompilerParams(collective_id=1, has_side_effects=True),
+        compiler_params=pltpu.CompilerParams(
+            collective_id=1, has_side_effects=True, vmem_limit_bytes=STEP_VMEM
+        ),
         cost_estimate=pl.CostEstimate(
             flops=12 * steps * PACK * height * width * (2 * width + 2 * height),
             transcendentals=0,
@@ -640,6 +654,7 @@
     packed_first, ocean_state, atmos_state = hold((packed_first, ocean_state, atmos_state))
     kernels_first = exchanged(packed_first)
     packed_rest = pack_filter(spectral_filter, lat_count, 2, 1, groups - 1)
+    packed_rest, ocean_state, flux_readout = hold((packed_rest, ocean_state, flux_readout))
     up = [(i, (i + 1) % lat_count) for i in range(lat_count)]
     down = [(j, i) for i, j in up]
     partial_flux = jnp.einsum("fc,chw->fhw", flux_readout, atmos_state, precision=EXACT)
@@ -657,8 +672,11 @@
         jnp.concatenate([by_rows[:, :2], jnp.broadcast_to(weight_up, closing.shape)], axis=1),
         mask[:2],
     )
-    rows_before = lax.ppermute(ocean_state[:, -2:], "lat", up)
-    rows_after = lax.ppermute(ocean_state[:, :2], "lat", down)
+    to_below, to_above, rows_last, rows_first = hold(
+        (to_below, to_above, ocean_state[:, -2:], ocean_state[:, :2])
+    )
+    rows_before = lax.ppermute(rows_last, "lat", up)
+    rows_after = lax.ppermute(rows_first, "lat", down)
     from_above = lax.ppermute(to_below, "lat", up)
     from_below = lax.ppermute(to_above, "lat", down)
     kernels_rest = exchanged(packed_rest)
@@ -735,13 +753,14 @@
     aside = ((0, 0), (RIM - 2, 24 - RIM - 2))
     field = jnp.pad(jnp.transpose(padded_field, (1, 2, 0)), aside + ((0, 0),))
     mask_field = jnp.pad(mask_rim, aside)[:, :, None]
-    small = (jnp.transpose(depth_taps, (0, 2, 1)), block_gain[:, None], layer_scale[:, None])
+    reduce_flat = jnp.swapaxes(reduce_weight, 1, 2)
+    small = (jnp.transpose(depth_taps, (0, 2, 1)), block_gain, layer_scale)
 
     kernels_first, kernels_rest, normed, field, surface_atmos = hold(
         (kernels_first, kernels_rest, normed, field, surface_atmos)
     )
     filtered, ocean_rows_next = spectral_step(
-        normed, kernels_first, kernels_rest, expand_weight, reduce_weight, field, mask_field, *small
+        normed, kernels_first, kernels_rest, expand_weight, reduce_flat, field, mask_field, *small
     )
     ocean_next = jnp.transpose(ocean_rows_next, (2, 0, 1))
     by_half = atmos_state.reshape(halves + (atm_rows, width_atm))

time: 312 us -> 295 us (0.946)
  waiting for transfers between devices: 25 us -> 50.4 us
  local copies, waits for them, and re-layouts: 43.2 us -> 27.6 us
  other arithmetic: 37.4 us -> 26.6 us
  Pallas kernels: 167 us -> 159 us
  matrix products: 9.69 us -> 5.79 us
    all_to_all x2, waiting for transfers between devices: 24.1 us -> 49.2 us  [exchanged(): return lax.all_to_all(x, 'lat', split_axis=0, concat_axis=0, tiled=True)]
    unnamed x27 -> x64, local copies, waits for them, and re-layouts: 7.73 us -> 16.1 us
    pallas_call x2, Pallas kernels: 10.3 us -> 5.74 us  [pack_filter(): pl.pallas_call(pack_kernel, out_shape=jax.ShapeDtypeStruct((lat_count, pa...]
    pallas_call x1, Pallas kernels: 157 us -> 153 us  [spectral_step(): pl.pallas_call(spectral_kernel, out_shape=(jax.ShapeDtypeStruct(normed.sh...]
  transfers between devices with their start and end apart: 12 -> 12, of which waited for: 2 -> 3; matrix products, arithmetic and copies ran while one was open for 23% -> 10% of each run, Pallas kernels for 2% -> 0%
where the time goes in v2:
time: 295 us; the launch traced here: 294 us
  Pallas kernels  159 us (54%)
  waiting for transfers between devices  50.4 us (17%)
  local copies, waits for them, and re-layouts  27.6 us (9%)
  other arithmetic  26.6 us (9%)
  starting transfers between devices  23.8 us (8%)
  matrix products  5.79 us (2%)
    pallas_call x1, Pallas kernels, spectral_step(): pl.pallas_call(spectral_kernel, out_shape=(jax.ShapeDtypeStruct(normed.sh...  153 us
    all_to_all x2, waiting for transfers between devices, exchanged(): return lax.all_to_all(x, 'lat', split_axis=0, concat_axis=0, tiled=True)  49.2 us
    unnamed x64, local copies, waits for them, and re-layouts  16.1 us
    all_to_all x2, starting transfers between devices, exchanged(): return lax.all_to_all(x, 'lat', split_axis=0, concat_axis=0, tiled=True)  8.2 us
  transfers between devices with their start and end apart: 12, of which 3 were waited for; matrix products, arithmetic and copies ran while one was open for 10% of the time, Pallas kernels for 0%

profile of v2, /device:TPU:0, one launch (start us, length us, event | category | flops | bytes accessed | tf_op | source)
XLA Modules:
  0.0 294.1 jit_solution(15635281947536733524)
XLA Ops:
  0.7 3.7 %copy-done.1 = f32[2,96,96,96]{3,2,1,0:T(8,128)S(1)} copy-done((f32[2,96,96,96]{3,2,1,0:T(8,128)S(1)}, f32[2,96,96,96]{3,2,1,0:T(8,128)}, u32[]{:S(2)}) %copy-start.1) | copy-done | bytes 7077912
  4.3 2.0 shard_map.221
  6.3 3.8 %shard_map.222 = f32[4,2,2,3,96,128]{5,4,3,2,1,0:T(8,128)} custom-call(s32[1]{0:T(128)} %bitcast.member_ref, f32[2,4,2,3,4,96,96]{6,5,4,3,2,1,0:T(8,128)S(1)} %bitcast.123), custom_call_target="tpu_custom_call" | custom-call | bytes 7077888 | tf_op jit(solution)/shard_map/pallas_call | solution.py:178
  10.1 0.7 broadcast_subtract_fusion.1
  10.8 0.6 slice_bitcast_fusion.21
  11.4 0.5 reduce_sum.54
  11.9 0.7 broadcast_divide_fusion.2
  12.6 2.2 fusion
  15.1 0.5 slice.187
  15.6 0.7 convert_element_type.11
  16.3 1.3 fusion.60
  17.7 1.2 copy.71
  18.9 0.8 fusion.58
  19.8 3.1 %collective-permute-start = (f32[9,3,384]{2,1,0:T(4,128)S(1)}, f32[9,3,384]{2,1,0:T(4,128)S(1)}, u32[]{:S(2)}, u32[]{:S(2)}) collective-permute-start(f32[9,3,384]{2,1,0:T(4,128)S(1)} %pad_maximum_fusion.4), channel_id=1, source_target_pairs={{0,4},{4,8},{8,12},{12,0},{1,5},{5,9},{9,13},{13,1},{2,6},{6,10},{... | collective-permute-start | bytes 124424 | tf_op jit(solution)/shard_map/ppermute | solution.py:680
  22.9 2.1 collective-permute-start.1
  25.0 3.8 %collective-permute-start.5 = (f32[200,2,128]{0,2,1:T(8,128)}, f32[200,2,128]{0,2,1:T(8,128)S(1)}, u32[]{:S(2)}, u32[]{:S(2)}) collective-permute-start(f32[200,2,128]{0,2,1:T(8,128)} %get-tuple-element.33), channel_id=1, source_target_pairs={{4,0},{8,4},{12,8},{0,12},{5,1},{9,5},{13,9},{1,13},{6,2},{10,6},{... | collective-permute-start | bytes 614408 | tf_op jit(solution)/shard_map/ppermute | solution.py:679
  28.8 3.5 %all-to-all-start = ((f32[4,2,1,3,96,128]{5,4,3,2,1,0:T(8,128)}), f32[4,2,1,3,96,128]{5,4,3,2,1,0:T(8,128)S(1)}, u32[]{:S(2)}, u32[]{:S(2)}) async-start(f32[4,2,1,3,96,128]{5,4,3,2,1,0:T(8,128)} %shard_map.221), calls=%async_computation | async-start | bytes 2359296 | tf_op jit(solution)/shard_map/all_to_all | solution.py:477
  32.4 2.4 fusion.57
  34.9 0.6 slice_bitcast_fusion.8
  35.8 0.6 copy.96
  36.4 0.7 fusion.59
  37.2 0.6 fusion.37
  38.0 0.6 maximum_bitcast_fusion
  38.6 0.9 copy.76
  39.5 1.1 collective-permute-done.5
  40.9 1.7 collective-permute-start.7
  42.6 1.0 fusion.56
  43.6 2.0 collective-permute-start.3
  45.6 1.6 pad_maximum_fusion
  47.2 0.7 reduce_sum.59
  48.0 0.7 reduce_sum.58
  48.7 0.7 broadcast_divide_fusion
  49.4 0.7 broadcast_divide_fusion.1
  50.0 0.7 broadcast_subtract_fusion
  50.7 0.7 and_select_fusion
  51.4 13.5 %all-to-all-done.first_ref = f32[4,2,1,3,96,128]{5,4,3,2,1,0:T(8,128)S(1)} async-done(((f32[4,2,1,3,96,128]{5,4,3,2,1,0:T(8,128)}), f32[4,2,1,3,96,128]{5,4,3,2,1,0:T(8,128)S(1)}, u32[]{:S(2)}, u32[]{:S(2)}) %all-to-all-start) | async-done | bytes 1179680 | tf_op jit(solution)/shard_map/all_to_all | solution.py:477
  64.9 4.7 %all-to-all-start.1 = ((f32[4,2,2,3,96,128]{5,4,3,2,1,0:T(8,128)}), f32[4,2,2,3,96,128]{5,4,3,2,1,0:T(8,128)}, u32[]{:S(2)}, u32[]{:S(2)}) async-start(f32[4,2,2,3,96,128]{5,4,3,2,1,0:T(8,128)} %shard_map.222), calls=%async_computation.1 | async-start | bytes 4718592 | tf_op jit(solution)/shard_map/all_to_all | solution.py:477
  69.6 1.7 fusion.7
  71.8 0.4 dynamic_update_slice.5
  72.2 0.5 slice_reduce_fusion
  72.9 1.1 copy.81.mask_ref
  74.0 0.4 slice_reduce_fusion.1
  74.5 1.0 dynamic-slice_add_fusion
  75.5 1.5 add.94
  77.0 2.6 collective-permute-start.9
  79.6 1.0 add.84
  80.6 0.4 fusion.11
  81.0 2.5 multiply_multiply_fusion
  83.5 0.8 fusion.4
  84.3 1.2 pad.23.field_ref
  85.5 1.6 add.95
  87.1 35.7 %all-to-all-done.1.rest_ref = f32[4,2,2,3,96,128]{5,4,3,2,1,0:T(8,128)} async-done(((f32[4,2,2,3,96,128]{5,4,3,2,1,0:T(8,128)}), f32[4,2,2,3,96,128]{5,4,3,2,1,0:T(8,128)}, u32[]{:S(2)}, u32[]{:S(2)}) %all-to-all-start.1) | async-done | bytes 2359328 | tf_op jit(solution)/shard_map/all_to_all | solution.py:477
  122.8 1.5 slice_bitcast_fusion.4
  124.3 1.3 copy-done.3
  125.6 1.3 copy-done.5
  126.9 1.1 copy-done.6
  128.0 0.8 copy-done.8
  128.7 1.4 copy-done.9
  130.1 1.4 copy-done.10
  131.5 153.0 %shard_map.223 = (f32[4,2,12,24,384]{4,3,2,1,0:T(8,128)S(1)}, f32[4,128,200]{2,1,0:T(8,128)S(1)}) custom-call(f32[4,2,12,24,384]{4,3,2,1,0:T(8,128)S(1)} %bitcast.124, f32[4,2,1,3,96,128]{5,4,3,2,1,0:T(8,128)S(1)} %copy-done.5, f32[4,2,2,3,96,128]{5,4,3,2,1,0:T(8,128)} %all-to-all-done.1.rest_ref, f32[2,200,800]{2,1,0:T(8,128)S(1)} %copy-done.9, ...), custom_call_target="tpu_custom_call" | custom-call | flops 10192158720 | bytes 10616832 | tf_op jit(solution)/shard_map/pallas_call | solution.py:433
  284.5 1.8 copy-done.2
  286.3 0.8 copy-done.7
  287.1 2.0 copy.86
  289.1 5.1 %add_add_fusion = f32[4,2,12,24,384]{4,3,2,1,0:T(8,128)} fusion(f32[4,2,12,24,384]{4,3,2,1,0:T(8,128)} %bitcast.128, f32[4,2,12,24,384]{4,3,2,1,0:T(8,128)} %copy-done.2, f32[24,384]{1,0:T(8,128)} %get-tuple-element.66, f32[4,2,12]{2,1,0:T(2,128)} %get-tuple-element.74, f32[24,384]{1,0:T(8,128)} %get-tuple-element.67, f32[4,2,12]{2,1,0:T(2,128)} %get-tuple-element.75, ...), kind=kLoop, calls=%fused_computation.2 | loop fusion | flops 7962624 | bytes 10765824 | tf_op jit(solution)/shard_map/add | solution.py:769
  (106 shorter events, 2.0 us)
Async XLA Ops:
  0.6 82.9 %copy-start = (f32[200,8]{0,1:T(8,128)S(1)}, f32[200,8]{0,1:T(8,128)}, u32[]{:S(2)}) copy-start(f32[200,8]{0,1:T(8,128)} %param.30) | copy-start | bytes 19204
  0.7 3.7 %copy-start.1 = (f32[2,96,96,96]{3,2,1,0:T(8,128)S(1)}, f32[2,96,96,96]{3,2,1,0:T(8,128)}, u32[]{:S(2)}) copy-start(f32[2,96,96,96]{3,2,1,0:T(8,128)} %param.25) | copy-start | bytes 21233668
  6.3 5.1 %copy-start.25 = (f32[4,2]{0,1:T(2,128)S(1)}, f32[4,2]{0,1:T(2,128)}, u32[]{:S(2)}) copy-start(f32[4,2]{0,1:T(2,128)} %param.36) | copy-start | bytes 100
  6.3 6.3 %copy-start.13 = (f32[96,24,384]{2,1,0:T(8,128)S(1)}, f32[96,24,384]{2,1,0:T(8,128)}, u32[]{:S(2)}) copy-start(f32[96,24,384]{2,1,0:T(8,128)} %param.22) | copy-start | bytes 10616836
  6.3 6.3 %copy-start.24 = (f32[8,96]{1,0:T(8,128)S(1)}, f32[8,96]{1,0:T(8,128)}, u32[]{:S(2)}) copy-start(f32[8,96]{1,0:T(8,128)} %param.27) | copy-start | bytes 9220
  11.9 2.9 copy-start.27
  11.9 2.9 copy-start.28
  14.8 2.9 copy-start.17
  18.9 15.9 %copy-start.29 = (s32[128,2]{0,1:T(2,128)S(1)}, s32[128,2]{0,1:T(2,128)}, u32[]{:S(2)}) copy-start(s32[128,2]{0,1:T(2,128)} %param.37) | copy-start | bytes 3076
  18.9 15.9 %copy-start.26 = (f32[96,4]{0,1:T(4,128)S(1)}, f32[96,4]{0,1:T(4,128)}, u32[]{:S(2)}) copy-start(f32[96,4]{0,1:T(4,128)} %param.28) | copy-start | bytes 4612
  18.9 16.6 %copy-start.30 = (f32[128,2]{0,1:T(2,128)S(1)}, f32[128,2]{0,1:T(2,128)}, u32[]{:S(2)}) copy-start(f32[128,2]{0,1:T(2,128)} %param.38) | copy-start | bytes 3076
  19.7 16.0 %copy-start.23 = (f32[2,200,9]{1,0,2:T(2,128)S(1)}, f32[2,200,9]{1,0,2:T(2,128)}, u32[]{:S(2)}) copy-start(f32[2,200,9]{1,0,2:T(2,128)} %param.39) | copy-start | bytes 43204
  19.8 17.4 %collective-permute-start = (f32[9,3,384]{2,1,0:T(4,128)S(1)}, f32[9,3,384]{2,1,0:T(4,128)S(1)}, u32[]{:S(2)}, u32[]{:S(2)}) collective-permute-start(f32[9,3,384]{2,1,0:T(4,128)S(1)} %pad_maximum_fusion.4), channel_id=1, source_target_pairs={{0,4},{4,8},{8,12},{12,0},{1,5},{5,9},{9,13},{13,1},{2,6},{6,10},{... | collective-permute-start | bytes 124424 | tf_op jit(solution)/shard_map/ppermute | solution.py:680
  22.9 13.5 %collective-permute-start.1 = (f32[9,3,384]{2,0,1:T(8,128)S(1)}, f32[9,3,384]{2,0,1:T(8,128)S(1)}, u32[]{:S(2)}, u32[]{:S(2)}) collective-permute-start(f32[9,3,384]{2,0,1:T(8,128)S(1)} %pad_maximum_fusion.2), channel_id=1, source_target_pairs={{4,0},{8,4},{12,8},{0,12},{5,1},{9,5},{13,9},{1,13},{6,2},{10,6},{... | collective-permute-start | bytes 124424 | tf_op jit(solution)/shard_map/ppermute | solution.py:681
  25.0 14.5 %collective-permute-start.4 = (f32[200,2,128]{0,2,1:T(8,128)}, f32[200,2,128]{0,2,1:T(8,128)S(1)}, u32[]{:S(2)}, u32[]{:S(2)}) collective-permute-start(f32[200,2,128]{0,2,1:T(8,128)} %get-tuple-element.32), channel_id=1, source_target_pairs={{0,4},{4,8},{8,12},{12,0},{1,5},{5,9},{9,13},{13,1},{2,6},{6,10},{... | collective-permute-start | bytes 614408 | tf_op jit(solution)/shard_map/ppermute | solution.py:678
  25.0 15.7 %collective-permute-start.5 = (f32[200,2,128]{0,2,1:T(8,128)}, f32[200,2,128]{0,2,1:T(8,128)S(1)}, u32[]{:S(2)}, u32[]{:S(2)}) collective-permute-start(f32[200,2,128]{0,2,1:T(8,128)} %get-tuple-element.33), channel_id=1, source_target_pairs={{4,0},{8,4},{12,8},{0,12},{5,1},{9,5},{13,9},{1,13},{6,2},{10,6},{... | collective-permute-start | bytes 614408 | tf_op jit(solution)/shard_map/ppermute | solution.py:679
  28.8 36.1 %all-to-all-start = ((f32[4,2,1,3,96,128]{5,4,3,2,1,0:T(8,128)}), f32[4,2,1,3,96,128]{5,4,3,2,1,0:T(8,128)S(1)}, u32[]{:S(2)}, u32[]{:S(2)}) async-start(f32[4,2,1,3,96,128]{5,4,3,2,1,0:T(8,128)} %shard_map.221), calls=%async_computation | async-start | bytes 2359296 | tf_op jit(solution)/shard_map/all_to_all | solution.py:477
  35.5 2.5 copy-start.20
  37.9 4.7 %collective-permute-start.2 = (f32[112,384]{1,0:T(8,128)S(1)}, f32[112,384]{1,0:T(8,128)}, u32[]{:S(2)}, u32[]{:S(2)}) collective-permute-start(f32[112,384]{1,0:T(8,128)S(1)} %pad_maximum_fusion.1), channel_id=1, source_target_pairs={{0,1},{1,0},{2,3},{3,2},{4,5},{5,4},{6,7},{7,6},{8,9},{9,8},{10,11... | collective-permute-start | bytes 516104 | tf_op jit(solution)/shard_map/ppermute | solution.py:483
  39.5 6.1 %copy-start.16 = (f32[1,8,128]{0,2,1:T(8,128)}, f32[1,8,128]{0,2,1:T(8,128)S(1)}, u32[]{:S(2)}) copy-start(f32[1,8,128]{0,2,1:T(8,128)S(1)} %copy.76) | copy-start | bytes 12292
  39.5 6.1 %copy-start.18 = (f32[200,2,128]{0,2,1:T(8,128)}, f32[200,2,128]{0,2,1:T(8,128)S(1)}, u32[]{:S(2)}) copy-start(f32[200,2,128]{0,2,1:T(8,128)S(1)} %collective-permute-done.4) | copy-start | bytes 614404
  40.7 4.9 %copy-start.19 = (f32[200,2,128]{0,2,1:T(8,128)}, f32[200,2,128]{0,2,1:T(8,128)S(1)}, u32[]{:S(2)}) copy-start(f32[200,2,128]{0,2,1:T(8,128)S(1)} %collective-permute-done.5) | copy-start | bytes 614404
  40.8 4.8 %collective-permute-start.6 = (f32[202,8,2]{0,2,1:T(2,128)S(1)}, f32[202,8,2]{0,2,1:T(2,128)S(1)}, u32[]{:S(2)}, u32[]{:S(2)}) collective-permute-start(f32[202,8,2]{0,2,1:T(2,128)S(1)} %get-tuple-element.59), channel_id=1, source_target_pairs={{0,1},{1,2},{2,3},{3,0},{4,5},{5,6},{6,7},{7,4},{8,9},{9,10},{10,1... | collective-permute-start | bytes 38792 | tf_op jit(solution)/shard_map/ppermute | solution.py:32
  40.9 4.8 %collective-permute-start.7 = (f32[202,8,2]{0,2,1:T(2,128)S(1)}, f32[202,8,2]{0,2,1:T(2,128)S(1)}, u32[]{:S(2)}, u32[]{:S(2)}) collective-permute-start(f32[202,8,2]{0,2,1:T(2,128)S(1)} %get-tuple-element.60), channel_id=1, source_target_pairs={{1,0},{2,1},{3,2},{0,3},{5,4},{6,5},{7,6},{4,7},{9,8},{10,9},{11,1... | collective-permute-start | bytes 38792 | tf_op jit(solution)/shard_map/ppermute | solution.py:33
  43.6 36.0 %collective-permute-start.3 = (f32[112,384]{1,0:T(8,128)S(1)}, f32[112,384]{1,0:T(8,128)}, u32[]{:S(2)}, u32[]{:S(2)}) collective-permute-start(f32[112,384]{1,0:T(8,128)S(1)} %fusion.56), channel_id=1, source_target_pairs={{0,2},{2,0},{1,3},{3,1},{4,6},{6,4},{5,7},{7,5},{8,10},{10,8},{9,1... | collective-permute-start | bytes 516104 | tf_op jit(solution)/shard_map/ppermute | solution.py:483
  47.2 26.8 %copy-start.14 = (f32[202,8,132]{0,2,1:T(8,128)}, f32[202,8,132]{0,2,1:T(8,128)S(1)}, u32[]{:S(2)}) copy-start(f32[202,8,132]{0,2,1:T(8,128)S(1)} %pad_maximum_fusion) | copy-start | bytes 2559748
  64.9 9.1 %copy-start.4 = (f32[4,2,1,3,96,128]{5,4,3,2,1,0:T(8,128)}, f32[4,2,1,3,96,128]{5,4,3,2,1,0:T(8,128)S(1)}, u32[]{:S(2)}) copy-start(f32[4,2,1,3,96,128]{5,4,3,2,1,0:T(8,128)S(1)} %all-to-all-done.first_ref) | copy-start | bytes 3538948
  64.9 57.9 %all-to-all-start.1 = ((f32[4,2,2,3,96,128]{5,4,3,2,1,0:T(8,128)}), f32[4,2,2,3,96,128]{5,4,3,2,1,0:T(8,128)}, u32[]{:S(2)}, u32[]{:S(2)}) async-start(f32[4,2,2,3,96,128]{5,4,3,2,1,0:T(8,128)} %shard_map.222), calls=%async_computation.1 | async-start | bytes 4718592 | tf_op jit(solution)/shard_map/all_to_all | solution.py:477
  72.2 2.3 collective-permute-start.8
  72.8 8.1 %copy-start.21 = (f32[8,132]{1,0:T(8,128)}, f32[8,132]{1,0:T(8,128)S(1)}, u32[]{:S(2)}) copy-start(f32[8,132]{1,0:T(8,128)S(1)} %slice_reduce_fusion) | copy-start | bytes 12676
  77.0 8.5 %collective-permute-start.9 = (f32[4,24,384]{2,1,0:T(8,128)}, f32[4,24,384]{2,1,0:T(8,128)S(1)}, u32[]{:S(2)}, u32[]{:S(2)}) collective-permute-start(f32[4,24,384]{2,1,0:T(8,128)} %add.94), channel_id=1, source_target_pairs={{0,2},{2,0},{1,3},{3,1},{4,6},{6,4},{5,7},{7,5},{8,10},{10,8},{9,1... | collective-permute-start | bytes 442376 | tf_op jit(solution)/shard_map/ppermute | solution.py:483
  80.9 2.6 copy-start.15
  80.9 2.6 copy-start.22
  83.5 40.8 %copy-start.11 = (f32[2,200]{1,0:T(2,128)S(1)}, f32[2,200]{1,0:T(2,128)}, u32[]{:S(2)}) copy-start(f32[2,200]{1,0:T(2,128)} %gain_ref.1) | copy-start | bytes 4804
  83.5 40.8 %copy-start.12 = (f32[2,200]{1,0:T(2,128)S(1)}, f32[2,200]{1,0:T(2,128)}, u32[]{:S(2)}) copy-start(f32[2,200]{1,0:T(2,128)} %scale_ref.1) | copy-start | bytes 4804
  124.3 1.3 copy-start.3
  125.6 1.3 copy-start.5
  126.9 1.1 copy-start.6
  128.0 0.8 copy-start.8
  128.7 1.4 copy-start.9
  130.1 1.4 copy-start.10
  284.5 1.8 copy-start.2
  286.3 0.8 copy-start.7
